TPU v7x, 512 devices: a whole 4x8x8 slice. The times are simulated.
512 devices in a mesh: tm: 32 (over y, z_hi, core), space: 16 (over x, z_lo).
Axes of the slice: x: 4, y: 8, z: 8 (z_hi: 2, z_lo: 4; z = z_hi * 4 + z_lo), core: 2. Of those that a mesh axis runs over, the one named last changes fastest.
Arguments:
- opening_guess_profile: float32 [32, 64, 128, 256], P('tm', 'space'), may hold values from -6 to 6
- capacity: float32 [64, 128, 256], P('space'), may hold values from 0.25 to 4
- thermal_forcing: float32 [32, 64, 128, 256], P('tm', 'space'), may hold values from -3 to 3
- rough_decay_factor: float32 [32, 64, 128, 256], P('tm', 'space'), may hold values from 0.2 to 1
- tile_ids: int32 [256, 128], P('tm', 'space'), may hold values from 0 to 2047, as said below
- tile_count: int32 [256, 16], P('tm', 'space'), may hold values from 2 to 8, as said below
- tile_blocks: float32 [256, 128, 64, 64], P('tm', 'space'), may hold values from -0.25 to 0.25
Outputs:
- updated_opening_state: float32 [32, 64, 128, 256], P('tm', 'space')
- accurate_ending_thermal_state: float32 [32, 64, 128, 256], P('tm', 'space')
Inputs may be any that keep to these rules, and one draw needn't show every extreme that they name: `tile_ids`: the 8 entries of one brick for one step are distinct tile numbers of that brick. `tile_count`: on every brick of every slab some step uses all 8 slots.
All inputs are finite; a program needn't handle non-finite values.
Results may differ from a plain program's by a relative error of at most 0.0003.
Values sent between devices are 32-bit elements; how exact they have to be, the bound alone decides.
A program may use at most 128 MiB of HBM per device.

v0:
```python
import jax
import jax.numpy as jnp
from jax import lax
from jax.sharding import Mesh
from jax.sharding import PartitionSpec as P

INCREMENTS = 8
SWEEPS = 4
TM = ("tm_0", "tm_1", "tm_2")


COND = 1.0


def extended(cells, sides, width):
    for axis, dim in sides:
        count = lax.axis_size(axis)
        ends = count - 1
        head = lax.slice_in_dim(cells, 0, width, axis=dim)
        tail = lax.slice_in_dim(cells, cells.shape[dim] - width, cells.shape[dim], axis=dim)
        cells = jnp.concatenate(
            [
                lax.ppermute(tail, axis, [(i, (i + 1) % count) for i in range(ends)]),
                cells,
                lax.ppermute(head, axis, [((i + 1) % count, i) for i in range(ends)]),
            ],
            axis=dim,
        )
    return cells


def nothing_yet(x, identity):
    return jax.tree.map(
        lambda a, e: jnp.broadcast_to(jnp.asarray(e, a.dtype), a.shape), x, identity
    )


def carried_in(x, axes, combine, identity):
    before = start = nothing_yet(x, identity)
    total = x
    for axis in reversed(axes):
        length, position = (lax.axis_size(axis), lax.axis_index(axis))
        pieces = jax.tree.map(lambda part: lax.all_gather(part, axis), total)
        inside, total = (start, start)
        for k in range(length):
            passed = k < position
            total = combine(total, jax.tree.map(lambda part: part[k], pieces))
            inside = jax.tree.map(lambda new, old: jnp.where(passed, new, old), total, inside)
        before = combine(inside, before)
    return before


def beside_sum(wide):
    center = wide[1:-1]
    padded = jnp.pad(center, ((0, 0), (1, 1), (1, 1)))
    total = wide[2:] + wide[:-2]
    total = total + padded[:, 2:, 1:-1] + padded[:, :-2, 1:-1]
    return total + padded[:, 1:-1, 2:] + padded[:, 1:-1, :-2]


def interface_fix(field, previous, tile_rows, live_count, blocks):
    shape = field.shape
    tile_len = blocks.shape[-1]
    delta = (field - previous).reshape(-1, tile_len)
    picked = delta[tile_rows]
    fixes = jnp.einsum("src,sc->sr", blocks, picked, precision=lax.Precision.HIGHEST)
    live = (jnp.arange(tile_rows.shape[0]) < live_count)[:, None]
    fixes = jnp.where(live, fixes, 0.0)
    tiles = field.reshape(-1, tile_len).at[tile_rows].add(fixes)
    return tiles.reshape(shape)


def shards(
    opening_guess_profile,
    capacity,
    thermal_forcing,
    rough_decay_factor,
    tile_ids,
    tile_count,
    tile_blocks,
):
    opening_moment = opening_guess_profile[0]
    source = thermal_forcing[0]
    rough_estimate = rough_decay_factor[0]
    width = opening_moment.shape[0]
    stacked = jnp.stack([capacity, source])
    rims = extended(stacked, (("space", 1),), SWEEPS)
    broad_heat_capacity = rims[0]
    wide_source = rims[1]
    wide_inverse = 1.0 / (broad_heat_capacity + 6.0 * COND)
    first_cell = lax.axis_index("space") * width - SWEEPS
    position = first_cell + jnp.arange(width + 2 * SWEEPS)
    inside = ((position >= 0) & (position < width * lax.axis_size("space")))[:, None, None]

    def advance(previous):
        wide_previous = extended(previous, (("space", 0),), SWEEPS)
        wide_rhs = broad_heat_capacity * wide_previous + wide_source
        field = wide_previous
        for sweep_index in range(SWEEPS):
            padded_rows = jnp.pad(field, ((1, 1), (0, 0), (0, 0)))
            field = jnp.where(
                inside, (wide_rhs + COND * beside_sum(padded_rows)) * wide_inverse, 0.0
            )
        return field[SWEEPS : SWEEPS + width]

    def solitary_advance_routine(step_index, field):
        moved = advance(field)
        tile_rows = lax.dynamic_index_in_dim(tile_ids, step_index, 0, keepdims=False)
        live_count = lax.dynamic_index_in_dim(tile_count, step_index, 0, keepdims=False)[0]
        blocks = lax.dynamic_index_in_dim(tile_blocks, step_index, 0, keepdims=False)
        return interface_fix(moved, field, tile_rows, live_count, blocks)

    accurate_ending_thermal_state = lax.fori_loop(
        0, INCREMENTS, solitary_advance_routine, opening_moment
    )
    opening_window = lax.axis_index(TM) == 0
    own_scale = jnp.where(opening_window, 0.0, rough_estimate)
    own_shift = jnp.where(
        opening_window,
        accurate_ending_thermal_state,
        accurate_ending_thermal_state - rough_estimate * opening_moment,
    )

    def compose(prior_iterate, later):
        return (later[0] * prior_iterate[0], later[0] * prior_iterate[1] + later[1])

    scale, shift = carried_in(
        (own_scale, own_shift),
        TM,
        compose,
        (jnp.ones_like(rough_estimate), jnp.zeros_like(rough_estimate)),
    )
    updated_opening_state = scale * opening_moment + shift
    return (updated_opening_state[None], accurate_ending_thermal_state[None])


def solution(mesh):
    split = Mesh(
        mesh.devices.reshape(8, 2, 2, mesh.shape["space"]), ("tm_0", "tm_1", "tm_2", "space")
    )
    return jax.shard_map(
        shards,
        mesh=split,
        in_specs=(
            P(TM, "space", None, None),
            P("space", None, None),
            P(TM, "space", None, None),
            P(TM, "space", None, None),
            P(TM, "space"),
            P(TM, "space"),
            P(TM, "space", None, None),
        ),
        out_specs=(P(TM, "space", None, None), P(TM, "space", None, None)),
        check_vma=False,
    )
```

profile of v0, /device:TPU:1, one launch (start us, length us, event | category | flops | bytes accessed | tf_op | source)
XLA Modules:
  0.0 603.2 jit_solution(13667812011912099333)
XLA Ops:
  16.9 16.2 %collective-permute-done.2 = f32[2,4,128,256]{3,2,1,0:T(8,128)} collective-permute-done((f32[2,4,128,256]{3,2,1,0:T(8,128)S(1)}, f32[2,4,128,256]{3,2,1,0:T(8,128)}, u32[]{:S(2)}, u32[]{:S(2)}) %collective-permute-start.2) | collective-permute-done | bytes 1048608 | tf_op jit(solution)/shard_map/ppermute | solution.py:23
  33.1 30.3 %collective-permute-done.3 = f32[2,4,128,256]{3,2,1,0:T(8,128)} collective-permute-done((f32[2,4,128,256]{3,2,1,0:T(8,128)S(1)}, f32[2,4,128,256]{3,2,1,0:T(8,128)}, u32[]{:S(2)}, u32[]{:S(2)}) %collective-permute-start.3) | collective-permute-done | bytes 1048608 | tf_op jit(solution)/shard_map/ppermute | solution.py:25
  67.8 298.5 %while.16 = (s32[]{:T(128)}, f32[4,128,256]{2,1,0:T(8,128)S(1)}, f32[12,128,256]{2,1,0:T(8,128)}, f32[12,128,256]{2,1,0:T(8,128)}, f32[12,128,256]{2,1,0:T(8,128...) while((s32[]{:T(128)}, f32[4,128,256]{2,1,0:T(8,128)S(1)}, ...), condition=%wide.region_2.3_spmd.clone, body=%wide.region_0.2_spmd.clone.sunk | while | flops 12322898 | bytes 60572668 | solution.py:113
  73.4 7.4 %collective-permute-done = f32[4,128,256]{2,1,0:T(8,128)S(1)} collective-permute-done((f32[4,128,256]{2,1,0:T(8,128)S(1)}, f32[4,128,256]{2,1,0:T(8,128)S(1)}, u32[]{:S(2)}, u32[]{:S(2)}) %collective-permute-start) | collective-permute-done | bytes 524320 | tf_op jit(solution)/shard_map/while/body/eval_jaxpr/ppermute | solution.py:23
  80.9 15.6 %collective-permute-done.1 = f32[4,128,256]{2,1,0:T(8,128)S(1)} collective-permute-done((f32[4,128,256]{2,1,0:T(8,128)S(1)}, f32[4,128,256]{2,1,0:T(8,128)S(1)}, u32[]{:S(2)}, u32[]{:S(2)}) %collective-permute-start.1) | collective-permute-done | bytes 524320 | tf_op jit(solution)/shard_map/while/body/eval_jaxpr/ppermute | solution.py:25
  113.1 6.6 %collective-permute-done = f32[4,128,256]{2,1,0:T(8,128)S(1)} collective-permute-done((f32[4,128,256]{2,1,0:T(8,128)S(1)}, f32[4,128,256]{2,1,0:T(8,128)S(1)}, u32[]{:S(2)}, u32[]{:S(2)}) %collective-permute-start) | collective-permute-done | bytes 524320 | tf_op jit(solution)/shard_map/while/body/eval_jaxpr/ppermute | solution.py:23
  119.7 15.8 %collective-permute-done.1 = f32[4,128,256]{2,1,0:T(8,128)S(1)} collective-permute-done((f32[4,128,256]{2,1,0:T(8,128)S(1)}, f32[4,128,256]{2,1,0:T(8,128)S(1)}, u32[]{:S(2)}, u32[]{:S(2)}) %collective-permute-start.1) | collective-permute-done | bytes 524320 | tf_op jit(solution)/shard_map/while/body/eval_jaxpr/ppermute | solution.py:25
  154.3 7.0 %collective-permute-done = f32[4,128,256]{2,1,0:T(8,128)S(1)} collective-permute-done((f32[4,128,256]{2,1,0:T(8,128)S(1)}, f32[4,128,256]{2,1,0:T(8,128)S(1)}, u32[]{:S(2)}, u32[]{:S(2)}) %collective-permute-start) | collective-permute-done | bytes 524320 | tf_op jit(solution)/shard_map/while/body/eval_jaxpr/ppermute | solution.py:23
  161.4 15.0 %collective-permute-done.1 = f32[4,128,256]{2,1,0:T(8,128)S(1)} collective-permute-done((f32[4,128,256]{2,1,0:T(8,128)S(1)}, f32[4,128,256]{2,1,0:T(8,128)S(1)}, u32[]{:S(2)}, u32[]{:S(2)}) %collective-permute-start.1) | collective-permute-done | bytes 524320 | tf_op jit(solution)/shard_map/while/body/eval_jaxpr/ppermute | solution.py:25
  193.5 7.4 %collective-permute-done = f32[4,128,256]{2,1,0:T(8,128)S(1)} collective-permute-done((f32[4,128,256]{2,1,0:T(8,128)S(1)}, f32[4,128,256]{2,1,0:T(8,128)S(1)}, u32[]{:S(2)}, u32[]{:S(2)}) %collective-permute-start) | collective-permute-done | bytes 524320 | tf_op jit(solution)/shard_map/while/body/eval_jaxpr/ppermute | solution.py:23
  201.0 11.9 %collective-permute-done.1 = f32[4,128,256]{2,1,0:T(8,128)S(1)} collective-permute-done((f32[4,128,256]{2,1,0:T(8,128)S(1)}, f32[4,128,256]{2,1,0:T(8,128)S(1)}, u32[]{:S(2)}, u32[]{:S(2)}) %collective-permute-start.1) | collective-permute-done | bytes 524320 | tf_op jit(solution)/shard_map/while/body/eval_jaxpr/ppermute | solution.py:25
  230.1 7.4 %collective-permute-done = f32[4,128,256]{2,1,0:T(8,128)S(1)} collective-permute-done((f32[4,128,256]{2,1,0:T(8,128)S(1)}, f32[4,128,256]{2,1,0:T(8,128)S(1)}, u32[]{:S(2)}, u32[]{:S(2)}) %collective-permute-start) | collective-permute-done | bytes 524320 | tf_op jit(solution)/shard_map/while/body/eval_jaxpr/ppermute | solution.py:23
  237.5 11.9 %collective-permute-done.1 = f32[4,128,256]{2,1,0:T(8,128)S(1)} collective-permute-done((f32[4,128,256]{2,1,0:T(8,128)S(1)}, f32[4,128,256]{2,1,0:T(8,128)S(1)}, u32[]{:S(2)}, u32[]{:S(2)}) %collective-permute-start.1) | collective-permute-done | bytes 524320 | tf_op jit(solution)/shard_map/while/body/eval_jaxpr/ppermute | solution.py:25
  266.6 7.4 %collective-permute-done = f32[4,128,256]{2,1,0:T(8,128)S(1)} collective-permute-done((f32[4,128,256]{2,1,0:T(8,128)S(1)}, f32[4,128,256]{2,1,0:T(8,128)S(1)}, u32[]{:S(2)}, u32[]{:S(2)}) %collective-permute-start) | collective-permute-done | bytes 524320 | tf_op jit(solution)/shard_map/while/body/eval_jaxpr/ppermute | solution.py:23
  274.0 10.4 %collective-permute-done.1 = f32[4,128,256]{2,1,0:T(8,128)S(1)} collective-permute-done((f32[4,128,256]{2,1,0:T(8,128)S(1)}, f32[4,128,256]{2,1,0:T(8,128)S(1)}, u32[]{:S(2)}, u32[]{:S(2)}) %collective-permute-start.1) | collective-permute-done | bytes 524320 | tf_op jit(solution)/shard_map/while/body/eval_jaxpr/ppermute | solution.py:25
  301.6 7.4 %collective-permute-done = f32[4,128,256]{2,1,0:T(8,128)S(1)} collective-permute-done((f32[4,128,256]{2,1,0:T(8,128)S(1)}, f32[4,128,256]{2,1,0:T(8,128)S(1)}, u32[]{:S(2)}, u32[]{:S(2)}) %collective-permute-start) | collective-permute-done | bytes 524320 | tf_op jit(solution)/shard_map/while/body/eval_jaxpr/ppermute | solution.py:23
  309.0 9.9 %collective-permute-done.1 = f32[4,128,256]{2,1,0:T(8,128)S(1)} collective-permute-done((f32[4,128,256]{2,1,0:T(8,128)S(1)}, f32[4,128,256]{2,1,0:T(8,128)S(1)}, u32[]{:S(2)}, u32[]{:S(2)}) %collective-permute-start.1) | collective-permute-done | bytes 524320 | tf_op jit(solution)/shard_map/while/body/eval_jaxpr/ppermute | solution.py:25
  336.1 7.4 %collective-permute-done = f32[4,128,256]{2,1,0:T(8,128)S(1)} collective-permute-done((f32[4,128,256]{2,1,0:T(8,128)S(1)}, f32[4,128,256]{2,1,0:T(8,128)S(1)}, u32[]{:S(2)}, u32[]{:S(2)}) %collective-permute-start) | collective-permute-done | bytes 524320 | tf_op jit(solution)/shard_map/while/body/eval_jaxpr/ppermute | solution.py:23
  343.5 11.2 %collective-permute-done.1 = f32[4,128,256]{2,1,0:T(8,128)S(1)} collective-permute-done((f32[4,128,256]{2,1,0:T(8,128)S(1)}, f32[4,128,256]{2,1,0:T(8,128)S(1)}, u32[]{:S(2)}, u32[]{:S(2)}) %collective-permute-start.1) | collective-permute-done | bytes 524320 | tf_op jit(solution)/shard_map/while/body/eval_jaxpr/ppermute | solution.py:25
  368.7 16.5 %all-gather.18.cloned.1.call-done = f32[8,128,256]{2,1,0:T(8,128)} async-done(((f32[4,128,256]{2,1,0:T(8,128)}), f32[8,128,256]{2,1,0:T(8,128)}) %all-gather.18.cloned.1.call-update) | async-done | bytes 1048592 | tf_op jit(solution)/shard_map/all_gather | solution.py:43
  388.6 44.2 %all-gather.10.cloned.1.call-done = f32[2,4,128,256]{3,2,1,0:T(8,128)} async-done(((f32[1,4,128,256]{3,2,1,0:T(8,128)}), f32[2,4,128,256]{3,2,1,0:T(8,128)}) %all-gather.10.cloned.1.call-update) | async-done | bytes 1048592 | tf_op jit(solution)/shard_map/all_gather | solution.py:43
  432.8 43.3 %all-gather.14.cloned.1.call-done = f32[2,4,128,256]{3,2,1,0:T(8,128)} async-done(((f32[1,4,128,256]{3,2,1,0:T(8,128)}), f32[2,4,128,256]{3,2,1,0:T(8,128)}) %all-gather.14.cloned.1.call-update) | async-done | bytes 1048592 | tf_op jit(solution)/shard_map/all_gather | solution.py:43
  479.4 52.9 %all-gather.12.cloned.1.call-done = f32[8,4,128,256]{3,2,1,0:T(8,128)} async-done(((f32[1,4,128,256]{3,2,1,0:T(8,128)}), f32[8,4,128,256]{3,2,1,0:T(8,128)}) %all-gather.12.cloned.1.call-update) | async-done | bytes 4194320 | tf_op jit(solution)/shard_map/all_gather | solution.py:43
  532.2 58.1 %all-gather.16.cloned.1.call-done = f32[8,4,128,256]{3,2,1,0:T(8,128)} async-done(((f32[1,4,128,256]{3,2,1,0:T(8,128)}), f32[8,4,128,256]{3,2,1,0:T(8,128)}) %all-gather.16.cloned.1.call-update) | async-done | bytes 4194320 | tf_op jit(solution)/shard_map/all_gather | solution.py:43
  (269 shorter events, 166.5 us)
Async XLA Ops:
  7.2 361.6 %all-gather.8.cloned.1.call-start = ((), (), s32[]{:S(2)}) async-start(), calls=%async_computation | async-start | bytes 1572864 | tf_op jit(solution)/shard_map/all_gather | solution.py:43
  8.6 24.4 %collective-permute-start.2 = (f32[2,4,128,256]{3,2,1,0:T(8,128)S(1)}, f32[2,4,128,256]{3,2,1,0:T(8,128)}, u32[]{:S(2)}, u32[]{:S(2)}) collective-permute-start(f32[2,4,128,256]{3,2,1,0:T(8,128)S(1)} %pad_maximum_fusion.1), channel_id=1, source_target_pairs={{0,1},{1,2},{2,3},{3,4},{4,5},{5,6},{6,7},{7,8},{8,9},{9,10},{10,1... | collective-permute-start | bytes 3145736 | tf_op jit(solution)/shard_map/ppermute | solution.py:23
  14.6 48.8 %collective-permute-start.3 = (f32[2,4,128,256]{3,2,1,0:T(8,128)S(1)}, f32[2,4,128,256]{3,2,1,0:T(8,128)}, u32[]{:S(2)}, u32[]{:S(2)}) collective-permute-start(f32[2,4,128,256]{3,2,1,0:T(8,128)S(1)} %pad_maximum_fusion.1), channel_id=1, source_target_pairs={{1,0},{2,1},{3,2},{4,3},{5,4},{6,5},{7,6},{8,7},{9,8},{10,9},{11,1... | collective-permute-start | bytes 3145736 | tf_op jit(solution)/shard_map/ppermute | solution.py:25
  16.8 368.5 %all-gather.18.cloned.1.call-start = ((), (), s32[]{:S(2)}) async-start(), calls=%async_computation.5 | async-start | bytes 1572864 | tf_op jit(solution)/shard_map/all_gather | solution.py:43
  67.8 13.0 %collective-permute-start = (f32[4,128,256]{2,1,0:T(8,128)S(1)}, f32[4,128,256]{2,1,0:T(8,128)S(1)}, u32[]{:S(2)}, u32[]{:S(2)}) collective-permute-start(f32[4,128,256]{2,1,0:T(8,128)S(1)} %get-tuple-element.359), channel_id=1, source_target_pairs={{0,1},{1,2},{2,3},{3,4},{4,5},{5,6},{6,7},{7,8},{8,9},{9,10},{10,1... | collective-permute-start | bytes 1572872 | tf_op jit(solution)/shard_map/while/body/eval_jaxpr/ppermute | solution.py:23
  70.0 26.5 %collective-permute-start.1 = (f32[4,128,256]{2,1,0:T(8,128)S(1)}, f32[4,128,256]{2,1,0:T(8,128)S(1)}, u32[]{:S(2)}, u32[]{:S(2)}) collective-permute-start(f32[4,128,256]{2,1,0:T(8,128)S(1)} %get-tuple-element.359), channel_id=1, source_target_pairs={{1,0},{2,1},{3,2},{4,3},{5,4},{6,5},{7,6},{8,7},{9,8},{10,9},{11,1... | collective-permute-start | bytes 1572872 | tf_op jit(solution)/shard_map/while/body/eval_jaxpr/ppermute | solution.py:25
  108.1 11.6 %collective-permute-start = (f32[4,128,256]{2,1,0:T(8,128)S(1)}, f32[4,128,256]{2,1,0:T(8,128)S(1)}, u32[]{:S(2)}, u32[]{:S(2)}) collective-permute-start(f32[4,128,256]{2,1,0:T(8,128)S(1)} %get-tuple-element.359), channel_id=1, source_target_pairs={{0,1},{1,2},{2,3},{3,4},{4,5},{5,6},{6,7},{7,8},{8,9},{9,10},{10,1... | collective-permute-start | bytes 1572872 | tf_op jit(solution)/shard_map/while/body/eval_jaxpr/ppermute | solution.py:23
  109.7 25.9 %collective-permute-start.1 = (f32[4,128,256]{2,1,0:T(8,128)S(1)}, f32[4,128,256]{2,1,0:T(8,128)S(1)}, u32[]{:S(2)}, u32[]{:S(2)}) collective-permute-start(f32[4,128,256]{2,1,0:T(8,128)S(1)} %get-tuple-element.359), channel_id=1, source_target_pairs={{1,0},{2,1},{3,2},{4,3},{5,4},{6,5},{7,6},{8,7},{9,8},{10,9},{11,1... | collective-permute-start | bytes 1572872 | tf_op jit(solution)/shard_map/while/body/eval_jaxpr/ppermute | solution.py:25
  147.2 14.1 %collective-permute-start = (f32[4,128,256]{2,1,0:T(8,128)S(1)}, f32[4,128,256]{2,1,0:T(8,128)S(1)}, u32[]{:S(2)}, u32[]{:S(2)}) collective-permute-start(f32[4,128,256]{2,1,0:T(8,128)S(1)} %get-tuple-element.359), channel_id=1, source_target_pairs={{0,1},{1,2},{2,3},{3,4},{4,5},{5,6},{6,7},{7,8},{8,9},{9,10},{10,1... | collective-permute-start | bytes 1572872 | tf_op jit(solution)/shard_map/while/body/eval_jaxpr/ppermute | solution.py:23
  150.9 25.4 %collective-permute-start.1 = (f32[4,128,256]{2,1,0:T(8,128)S(1)}, f32[4,128,256]{2,1,0:T(8,128)S(1)}, u32[]{:S(2)}, u32[]{:S(2)}) collective-permute-start(f32[4,128,256]{2,1,0:T(8,128)S(1)} %get-tuple-element.359), channel_id=1, source_target_pairs={{1,0},{2,1},{3,2},{4,3},{5,4},{6,5},{7,6},{8,7},{9,8},{10,9},{11,1... | collective-permute-start | bytes 1572872 | tf_op jit(solution)/shard_map/while/body/eval_jaxpr/ppermute | solution.py:25
  188.0 12.9 %collective-permute-start = (f32[4,128,256]{2,1,0:T(8,128)S(1)}, f32[4,128,256]{2,1,0:T(8,128)S(1)}, u32[]{:S(2)}, u32[]{:S(2)}) collective-permute-start(f32[4,128,256]{2,1,0:T(8,128)S(1)} %get-tuple-element.359), channel_id=1, source_target_pairs={{0,1},{1,2},{2,3},{3,4},{4,5},{5,6},{6,7},{7,8},{8,9},{9,10},{10,1... | collective-permute-start | bytes 1572872 | tf_op jit(solution)/shard_map/while/body/eval_jaxpr/ppermute | solution.py:23
  190.2 22.7 %collective-permute-start.1 = (f32[4,128,256]{2,1,0:T(8,128)S(1)}, f32[4,128,256]{2,1,0:T(8,128)S(1)}, u32[]{:S(2)}, u32[]{:S(2)}) collective-permute-start(f32[4,128,256]{2,1,0:T(8,128)S(1)} %get-tuple-element.359), channel_id=1, source_target_pairs={{1,0},{2,1},{3,2},{4,3},{5,4},{6,5},{7,6},{8,7},{9,8},{10,9},{11,1... | collective-permute-start | bytes 1572872 | tf_op jit(solution)/shard_map/while/body/eval_jaxpr/ppermute | solution.py:25
  224.5 12.9 %collective-permute-start = (f32[4,128,256]{2,1,0:T(8,128)S(1)}, f32[4,128,256]{2,1,0:T(8,128)S(1)}, u32[]{:S(2)}, u32[]{:S(2)}) collective-permute-start(f32[4,128,256]{2,1,0:T(8,128)S(1)} %get-tuple-element.359), channel_id=1, source_target_pairs={{0,1},{1,2},{2,3},{3,4},{4,5},{5,6},{6,7},{7,8},{8,9},{9,10},{10,1... | collective-permute-start | bytes 1572872 | tf_op jit(solution)/shard_map/while/body/eval_jaxpr/ppermute | solution.py:23
  226.7 22.7 %collective-permute-start.1 = (f32[4,128,256]{2,1,0:T(8,128)S(1)}, f32[4,128,256]{2,1,0:T(8,128)S(1)}, u32[]{:S(2)}, u32[]{:S(2)}) collective-permute-start(f32[4,128,256]{2,1,0:T(8,128)S(1)} %get-tuple-element.359), channel_id=1, source_target_pairs={{1,0},{2,1},{3,2},{4,3},{5,4},{6,5},{7,6},{8,7},{9,8},{10,9},{11,1... | collective-permute-start | bytes 1572872 | tf_op jit(solution)/shard_map/while/body/eval_jaxpr/ppermute | solution.py:25
  261.0 12.9 %collective-permute-start = (f32[4,128,256]{2,1,0:T(8,128)S(1)}, f32[4,128,256]{2,1,0:T(8,128)S(1)}, u32[]{:S(2)}, u32[]{:S(2)}) collective-permute-start(f32[4,128,256]{2,1,0:T(8,128)S(1)} %get-tuple-element.359), channel_id=1, source_target_pairs={{0,1},{1,2},{2,3},{3,4},{4,5},{5,6},{6,7},{7,8},{8,9},{9,10},{10,1... | collective-permute-start | bytes 1572872 | tf_op jit(solution)/shard_map/while/body/eval_jaxpr/ppermute | solution.py:23
  263.2 21.2 %collective-permute-start.1 = (f32[4,128,256]{2,1,0:T(8,128)S(1)}, f32[4,128,256]{2,1,0:T(8,128)S(1)}, u32[]{:S(2)}, u32[]{:S(2)}) collective-permute-start(f32[4,128,256]{2,1,0:T(8,128)S(1)} %get-tuple-element.359), channel_id=1, source_target_pairs={{1,0},{2,1},{3,2},{4,3},{5,4},{6,5},{7,6},{8,7},{9,8},{10,9},{11,1... | collective-permute-start | bytes 1572872 | tf_op jit(solution)/shard_map/while/body/eval_jaxpr/ppermute | solution.py:25
  296.0 12.9 %collective-permute-start = (f32[4,128,256]{2,1,0:T(8,128)S(1)}, f32[4,128,256]{2,1,0:T(8,128)S(1)}, u32[]{:S(2)}, u32[]{:S(2)}) collective-permute-start(f32[4,128,256]{2,1,0:T(8,128)S(1)} %get-tuple-element.359), channel_id=1, source_target_pairs={{0,1},{1,2},{2,3},{3,4},{4,5},{5,6},{6,7},{7,8},{8,9},{9,10},{10,1... | collective-permute-start | bytes 1572872 | tf_op jit(solution)/shard_map/while/body/eval_jaxpr/ppermute | solution.py:23
  298.2 20.7 %collective-permute-start.1 = (f32[4,128,256]{2,1,0:T(8,128)S(1)}, f32[4,128,256]{2,1,0:T(8,128)S(1)}, u32[]{:S(2)}, u32[]{:S(2)}) collective-permute-start(f32[4,128,256]{2,1,0:T(8,128)S(1)} %get-tuple-element.359), channel_id=1, source_target_pairs={{1,0},{2,1},{3,2},{4,3},{5,4},{6,5},{7,6},{8,7},{9,8},{10,9},{11,1... | collective-permute-start | bytes 1572872 | tf_op jit(solution)/shard_map/while/body/eval_jaxpr/ppermute | solution.py:25
  330.5 12.9 %collective-permute-start = (f32[4,128,256]{2,1,0:T(8,128)S(1)}, f32[4,128,256]{2,1,0:T(8,128)S(1)}, u32[]{:S(2)}, u32[]{:S(2)}) collective-permute-start(f32[4,128,256]{2,1,0:T(8,128)S(1)} %get-tuple-element.359), channel_id=1, source_target_pairs={{0,1},{1,2},{2,3},{3,4},{4,5},{5,6},{6,7},{7,8},{8,9},{9,10},{10,1... | collective-permute-start | bytes 1572872 | tf_op jit(solution)/shard_map/while/body/eval_jaxpr/ppermute | solution.py:23
  332.7 22.1 %collective-permute-start.1 = (f32[4,128,256]{2,1,0:T(8,128)S(1)}, f32[4,128,256]{2,1,0:T(8,128)S(1)}, u32[]{:S(2)}, u32[]{:S(2)}) collective-permute-start(f32[4,128,256]{2,1,0:T(8,128)S(1)} %get-tuple-element.359), channel_id=1, source_target_pairs={{1,0},{2,1},{3,2},{4,3},{5,4},{6,5},{7,6},{8,7},{9,8},{10,9},{11,1... | collective-permute-start | bytes 1572872 | tf_op jit(solution)/shard_map/while/body/eval_jaxpr/ppermute | solution.py:25
  368.7 64.1 %all-gather.10.cloned.1.call-start = ((), (), s32[]{:S(2)}) async-start(), calls=%async_computation.1 | async-start | bytes 1572864 | tf_op jit(solution)/shard_map/all_gather | solution.py:43
  387.9 88.2 %all-gather.14.cloned.1.call-start = ((), (), s32[]{:S(2)}) async-start(), calls=%async_computation.3 | async-start | bytes 1572864 | tf_op jit(solution)/shard_map/all_gather | solution.py:43
  388.5 143.7 %all-gather.12.cloned.1.call-start = ((), (), s32[]{:S(2)}) async-start(), calls=%async_computation.2 | async-start | bytes 4718592 | tf_op jit(solution)/shard_map/all_gather | solution.py:43
  478.8 111.6 %all-gather.16.cloned.1.call-start = ((), (), s32[]{:S(2)}) async-start(), calls=%async_computation.4 | async-start | bytes 4718592 | tf_op jit(solution)/shard_map/all_gather | solution.py:43
  (34 other events, 1288.5 us)
Sparse Core Ops, SparseCore 0:
  16.9 25.5 all-gather.7
  368.8 16.4 all-gather.17
  388.0 44.7 all-gather.9
  434.8 41.3 all-gather.13
  478.9 53.3 all-gather.11
  534.2 56.0 all-gather.15
where the time goes:
time: 605 us; the launch traced here: 603 us
  waiting for transfers between devices  422 us (70%)
  other arithmetic  80.9 us (13%)
  local copies, waits for them, and re-layouts  36.4 us (6%)
  starting transfers between devices  36.3 us (6%)
  between operations  14.3 us (2%)
  matrix products  11.8 us (2%)
    all_gather x6, waiting for transfers between devices, carried_in(): pieces = jax.tree.map(lambda part: lax.all_gather(part, axis), total)  215 us
    ppermute x9, waiting for transfers between devices, extended(): lax.ppermute(head, axis, [((i + 1) % count, i) for i in range(ends)])  132 us
    ppermute x9, waiting for transfers between devices, extended(): lax.ppermute(tail, axis, [(i, (i + 1) % count) for i in range(ends)])  74.1 us
    select_n x24, other arithmetic, advance(): jnp.where(inside, (wide_rhs + COND * beside_sum(padded_rows)) * wide_inve...  25.3 us
    ppermute x9, starting transfers between devices, extended(): lax.ppermute(tail, axis, [(i, (i + 1) % count) for i in range(ends)])  24.5 us
    gather x8, local copies, waits for them, and re-layouts, interface_fix(): picked = delta[tile_rows]  14.2 us
  transfers between devices with their start and end apart: 24, of which 23 were waited for; matrix products, arithmetic and copies ran while one was open for 19% of the time, Pallas kernels for 0%

commit v1 on v0

v1 whole, which is shorter than its diff:
```python
import jax
import jax.numpy as jnp
from jax import lax
from jax.experimental import pallas as pl
from jax.experimental.pallas import tpu as pltpu
from jax.sharding import Mesh
from jax.sharding import PartitionSpec as P

INCREMENTS = 8
SWEEPS = 4
TM = ("tm_0", "tm_1", "tm_2")
SPACE = ("sx", "sz")
MESH = pl.DeviceIdType.MESH
COND = 1.0

NZD = 4
NXD = 4
DEEP = 4
LAYERS = DEEP * NZD
ROWS = 32
NY = ROWS * NZD
NZ = 256
TILE = 64
MAXT = 8
PAIRS = MAXT // 2


def nothing_yet(x, identity):
    return jax.tree.map(
        lambda a, e: jnp.broadcast_to(jnp.asarray(e, a.dtype), a.shape), x, identity
    )


def carried_in(x, axes, combine, identity):
    before = start = nothing_yet(x, identity)
    total = x
    for axis in reversed(axes):
        length, position = (lax.axis_size(axis), lax.axis_index(axis))
        pieces = jax.tree.map(lambda part: lax.all_gather(part, axis), total)
        inside, total = (start, start)
        for k in range(length):
            passed = k < position
            total = combine(total, jax.tree.map(lambda part: part[k], pieces))
            inside = jax.tree.map(lambda new, old: jnp.where(passed, new, old), total, inside)
        before = combine(inside, before)
    return before


def fine_kernel(
    g_ref, c_ref, f_ref, ids_ref, cnt_ref, m_ref,
    e_ref,
    p, a, b, inv, cap, src, rhs, back,
    xlo, xhi, zlo, zhi, zs_lo, zs_hi, inv_lo, inv_hi,
    bt, idv, dx, ids_s,
    in_send, in_recv, id_send, id_recv, h_send, h_recv, b_send, b_recv, o_send, o_recv, loc,
):
    sx = lax.axis_index("sx")
    sz = lax.axis_index("sz")
    has_xl, has_xr = sx > 0, sx < NXD - 1
    has_zl, has_zr = sz > 0, sz < NZD - 1

    barrier = pltpu.get_barrier_semaphore()
    for o in range(1, NZD):
        pl.semaphore_signal(
            barrier, inc=1, device_id={"sz": lax.rem(sz + o, NZD)}, device_id_type=MESH
        )

    @pl.when(has_xl)
    def _():
        pl.semaphore_signal(barrier, inc=1, device_id={"sx": sx - 1}, device_id_type=MESH)

    @pl.when(has_xr)
    def _():
        pl.semaphore_signal(barrier, inc=1, device_id={"sx": sx + 1}, device_id_type=MESH)

    idv[sz] = jnp.zeros((INCREMENTS, 128), jnp.int32)
    idv[sz, :, 0:MAXT] = ids_ref[...]
    idv[sz, :, MAXT : MAXT + 1] = cnt_ref[...]
    for k in range(INCREMENTS):
        for i in range(PAIRS):
            two = m_ref[k, 2 * i : 2 * i + 2].reshape(2 * TILE, TILE)
            bt[k, sz, i] = two.T
    zero_x = jnp.zeros((2, ROWS, NZ), jnp.float32)
    zero_z = jnp.zeros((2, LAYERS, NZ), jnp.float32)

    @pl.when(jnp.logical_not(has_xl))
    def _():
        xlo[...] = zero_x

    @pl.when(jnp.logical_not(has_xr))
    def _():
        xhi[...] = zero_x

    @pl.when(jnp.logical_not(has_zl))
    def _():
        zlo[...] = zero_z

    @pl.when(jnp.logical_not(has_zr))
    def _():
        zhi[...] = zero_z

    pl.semaphore_wait(
        barrier, NZD - 1 + has_xl.astype(jnp.int32) + has_xr.astype(jnp.int32)
    )

    def dealt(n, o):
        to = lax.rem(sz + o, NZD)
        source = (g_ref.at[0], f_ref.at[0], c_ref)[n]
        target = (p, src, cap)[n]
        return pltpu.make_async_remote_copy(
            src_ref=source.at[:, pl.ds(ROWS * to, ROWS), :],
            dst_ref=target.at[pl.ds(DEEP * sz, DEEP)],
            send_sem=in_send.at[n, o],
            recv_sem=in_recv.at[n, o],
            device_id={"sz": to},
            device_id_type=MESH,
        )

    def listed(o):
        to = lax.rem(sz + o, NZD)
        return pltpu.make_async_remote_copy(
            src_ref=idv.at[sz],
            dst_ref=idv.at[sz],
            send_sem=id_send.at[o],
            recv_sem=id_recv.at[o],
            device_id={"sz": to},
            device_id_type=MESH,
        )

    for o in range(1, NZD):
        listed(o).start()
    for n in range(3):
        for o in range(1, NZD):
            dealt(n, o).start()

    def block_copy(k, d, r):
        brick = sz - r if d == 0 else sz + r
        return pltpu.make_async_remote_copy(
            src_ref=bt.at[k, jnp.clip(brick, 0, NZD - 1)],
            dst_ref=bt.at[k, jnp.clip(brick, 0, NZD - 1)],
            send_sem=b_send.at[lax.rem(k, 2), d, r],
            recv_sem=b_recv.at[lax.rem(k, 2), d, r],
            device_id={"sz": jnp.clip(sz + 1 if d == 0 else sz - 1, 0, NZD - 1)},
            device_id_type=MESH,
        )

    def block_start(k, r):
        @pl.when(jnp.logical_and(sz - r >= 0, has_zr))
        def _():
            block_copy(k, 0, r).start()

        @pl.when(jnp.logical_and(sz + r < NZD, has_zl))
        def _():
            block_copy(k, 1, r).start()

    def block_wait(k, r):
        @pl.when(jnp.logical_and(sz - r >= 0, has_zr))
        def _():
            block_copy(k, 0, r).wait_send()

        @pl.when(jnp.logical_and(sz + r < NZD, has_zl))
        def _():
            block_copy(k, 1, r).wait_send()

        @pl.when(sz - 1 - r >= 0)
        def _():
            block_copy(k, 0, r).wait_recv()

        @pl.when(sz + 1 + r < NZD)
        def _():
            block_copy(k, 1, r).wait_recv()

    block_start(0, 0)
    mine = pl.ds(DEEP * sz, DEEP)
    p[mine] = g_ref[0, :, pl.ds(ROWS * sz, ROWS), :]
    src[mine] = f_ref[0, :, pl.ds(ROWS * sz, ROWS), :]
    cap[mine] = c_ref[:, pl.ds(ROWS * sz, ROWS), :]
    for o in range(1, NZD):
        listed(o).wait()
    lists = pltpu.make_async_copy(idv, ids_s, loc)
    lists.start()
    for n in range(3):
        for o in range(1, NZD):
            dealt(n, o).wait()
    lists.wait()
    block_wait(0, 0)
    block_start(0, 1)

    for l in range(LAYERS):
        inv[l] = 1.0 / (cap[l] + 6.0 * COND)
    inv_lo[...] = inv[:, 0, :]
    inv_hi[...] = inv[:, ROWS - 1, :]
    zs_lo[0] = p[:, 0, :]
    zs_hi[0] = p[:, ROWS - 1, :]

    row = lax.broadcasted_iota(jnp.int32, (ROWS, NZ), 0)
    lane = lax.broadcasted_iota(jnp.int32, (ROWS, NZ), 1)

    def halo(field, slot):
        def copy(n, source, target, where):
            return pltpu.make_async_remote_copy(
                src_ref=source,
                dst_ref=target,
                send_sem=h_send.at[n, slot],
                recv_sem=h_recv.at[n, slot],
                device_id=where,
                device_id_type=MESH,
            )

        xl, xr = {"sx": jnp.maximum(sx - 1, 0)}, {"sx": jnp.minimum(sx + 1, NXD - 1)}
        zl, zr = {"sz": jnp.maximum(sz - 1, 0)}, {"sz": jnp.minimum(sz + 1, NZD - 1)}
        return (
            (has_xl, has_xr, lambda: copy(0, field.at[0], xhi.at[slot], xl)),
            (has_xr, has_xl, lambda: copy(1, field.at[LAYERS - 1], xlo.at[slot], xr)),
            (has_zl, has_zr, lambda: copy(2, zs_lo.at[slot], zhi.at[slot], zl)),
            (has_zr, has_zl, lambda: copy(3, zs_hi.at[slot], zlo.at[slot], zr)),
        )

    def sweep(old, new, slot, first, last, between):
        copies = halo(old, slot)
        for sends, unused, copy in copies:
            @pl.when(sends)
            def _(copy=copy):
                copy().start()

        between()
        for l in range(LAYERS):
            w = old[l]
            t = jnp.where(row == 0, 0.0, pltpu.roll(w, 1, 0))
            t = t + jnp.where(row == ROWS - 1, 0.0, pltpu.roll(w, ROWS - 1, 0))
            t = t + jnp.where(lane == 0, 0.0, pltpu.roll(w, 1, 1))
            t = t + jnp.where(lane == NZ - 1, 0.0, pltpu.roll(w, NZ - 1, 1))
            if l > 0:
                t = t + old[l - 1]
            if l < LAYERS - 1:
                t = t + old[l + 1]
            if first:
                r = cap[l] * w + src[l]
                rhs[l] = r
            else:
                r = rhs[l]
            new[l] = (r + COND * t) * inv[l]
        for sends, gets, copy in copies:
            @pl.when(sends)
            def _(copy=copy):
                copy().wait_send()

            @pl.when(gets)
            def _(copy=copy):
                copy().wait_recv()

        new[0] = new[0] + COND * (inv[0] * xlo[slot])
        new[LAYERS - 1] = new[LAYERS - 1] + COND * (inv[LAYERS - 1] * xhi[slot])
        lo = new[:, 0, :] + COND * (inv_lo[...] * zlo[slot])
        hi = new[:, ROWS - 1, :] + COND * (inv_hi[...] * zhi[slot])
        new[:, 0, :] = lo
        new[:, ROWS - 1, :] = hi
        if not last:
            zs_lo[1 - slot] = lo
            zs_hi[1 - slot] = hi

    lane_r = lax.broadcasted_iota(jnp.int32, (1, 128), 1) < TILE
    lane_c = lax.broadcasted_iota(jnp.int32, (TILE, 128), 1) < TILE
    cell = lax.broadcasted_iota(jnp.int32, (DEEP * ROWS, NZ), 0)

    def fix(k):
        places = []
        for brick in range(NZD):
            count = ids_s[brick, k, MAXT]
            for i in range(PAIRS):
                halves = []
                for odd in range(2):
                    slot = 2 * i + odd
                    tile = ids_s[brick, k, slot]
                    quad = lax.rem(tile, 4)
                    line = lax.rem(tile // 4, NY) - ROWS * sz
                    layer = tile // (4 * NY)
                    owned = (line >= 0) & (line < ROWS) & (slot < count)
                    line_in = jnp.clip(line, 0, ROWS - 1)
                    where = DEEP * brick + layer
                    d = b[where, pl.ds(line_in, 1), :] - p[where, pl.ds(line_in, 1), :]
                    h = jnp.where(quad >= 2, d[:, 128:], d[:, :128])
                    turn = lax.rem(quad, 2) != odd
                    h = jnp.where(turn, pltpu.roll(h, TILE, 1), h)
                    halves.append(h)
                    places.append((jnp.where(owned, layer * ROWS + line_in, -1), quad, turn))
                dx[brick * PAIRS + i : brick * PAIRS + i + 1, :] = jnp.where(
                    lane_r, halves[0], halves[1]
                )
        columns = dx[...].T
        for brick in range(NZD):
            total = b[DEEP * brick : DEEP * (brick + 1)].reshape(DEEP * ROWS, NZ)
            for i in range(PAIRS):
                at = brick * PAIRS + i
                d = jnp.where(
                    lane_c,
                    jnp.broadcast_to(columns[0:TILE, at : at + 1], (TILE, 128)),
                    jnp.broadcast_to(columns[TILE : 2 * TILE, at : at + 1], (TILE, 128)),
                )
                sums = jnp.sum(bt[k, brick, i] * d, axis=0, keepdims=True)
                for odd in range(2):
                    place, quad, turn = places[brick * MAXT + 2 * i + odd]
                    h = jnp.where(turn, pltpu.roll(sums, TILE, 1), sums)
                    right = lax.rem(quad, 2) == 1
                    h = jnp.where(lane_r != right, h, 0.0)
                    wide = jnp.concatenate(
                        [jnp.where(quad < 2, h, 0.0), jnp.where(quad < 2, 0.0, h)], axis=1
                    )
                    total = total + jnp.where(cell == place, wide, 0.0)
            p[DEEP * brick : DEEP * (brick + 1)] = total.reshape(DEEP, ROWS, NZ)
        zs_lo[0] = p[:, 0, :]
        zs_hi[0] = p[:, ROWS - 1, :]

    dx[...] = jnp.zeros((128, 128), jnp.float32)

    def step(k, carry):
        def one():
            block_wait(k, 1)
            block_start(k, 2)

        def three():
            @pl.when(k < INCREMENTS - 1)
            def _():
                block_start(k + 1, 0)

        def four():
            @pl.when(k < INCREMENTS - 1)
            def _():
                block_wait(k + 1, 0)
                block_start(k + 1, 1)

        sweep(p, a, 0, True, False, one)
        sweep(a, b, 1, False, False, lambda: None)
        sweep(b, a, 0, False, False, three)
        sweep(a, b, 1, False, True, four)
        block_wait(k, 2)
        fix(k)
        return carry

    lax.fori_loop(0, INCREMENTS, step, 0)

    def returned(o):
        to = lax.rem(sz + o, NZD)
        return pltpu.make_async_remote_copy(
            src_ref=p.at[pl.ds(DEEP * to, DEEP)],
            dst_ref=back.at[:, pl.ds(ROWS * sz, ROWS), :],
            send_sem=o_send.at[o],
            recv_sem=o_recv.at[o],
            device_id={"sz": to},
            device_id_type=MESH,
        )

    for o in range(1, NZD):
        returned(o).start()
    back[:, pl.ds(ROWS * sz, ROWS), :] = p[mine]
    for o in range(1, NZD):
        returned(o).wait()
    e_ref[0] = back[...]


def fine(g, c, f, ids, cnt, m):
    vm = pl.BlockSpec(memory_space=pltpu.VMEM)
    field = pltpu.VMEM((LAYERS, ROWS, NZ), jnp.float32)
    xf = pltpu.VMEM((2, ROWS, NZ), jnp.float32)
    zf = pltpu.VMEM((2, LAYERS, NZ), jnp.float32)
    z1 = pltpu.VMEM((LAYERS, NZ), jnp.float32)
    dma = pltpu.SemaphoreType.DMA
    return pl.pallas_call(
        fine_kernel,
        out_shape=jax.ShapeDtypeStruct(g.shape, jnp.float32),
        in_specs=[vm] * 6,
        out_specs=vm,
        scratch_shapes=[field] * 7
        + [pltpu.VMEM((DEEP, NY, NZ), jnp.float32)]
        + [xf, xf, zf, zf, zf, zf, z1, z1]
        + [
            pltpu.VMEM((INCREMENTS, NZD, PAIRS, TILE, 128), jnp.float32),
            pltpu.VMEM((NZD, INCREMENTS, 128), jnp.int32),
            pltpu.VMEM((128, 128), jnp.float32),
            pltpu.SMEM((NZD, INCREMENTS, 128), jnp.int32),
            dma((3, NZD)), dma((3, NZD)), dma((NZD,)), dma((NZD,)),
            dma((4, 2)), dma((4, 2)), dma((2, 2, 3)), dma((2, 2, 3)),
            dma((NZD,)), dma((NZD,)), dma,
        ],
        compiler_params=pltpu.CompilerParams(
            collective_id=0, has_side_effects=True, vmem_limit_bytes=48 << 20
        ),
    )(g, c, f, ids, cnt, m)


def shards(
    opening_guess_profile,
    capacity,
    thermal_forcing,
    rough_decay_factor,
    tile_ids,
    tile_count,
    tile_blocks,
):
    opening_moment = opening_guess_profile[0]
    rough_estimate = rough_decay_factor[0]
    accurate_ending_thermal_state = fine(
        opening_guess_profile, capacity, thermal_forcing, tile_ids, tile_count, tile_blocks
    )[0]
    opening_window = lax.axis_index(TM) == 0
    own_scale = jnp.where(opening_window, 0.0, rough_estimate)
    own_shift = jnp.where(
        opening_window,
        accurate_ending_thermal_state,
        accurate_ending_thermal_state - rough_estimate * opening_moment,
    )

    def compose(prior_iterate, later):
        return (later[0] * prior_iterate[0], later[0] * prior_iterate[1] + later[1])

    scale, shift = carried_in(
        (own_scale, own_shift),
        TM,
        compose,
        (jnp.ones_like(rough_estimate), jnp.zeros_like(rough_estimate)),
    )
    updated_opening_state = scale * opening_moment + shift
    return (updated_opening_state[None], accurate_ending_thermal_state[None])


def solution(mesh):
    split = Mesh(
        mesh.devices.reshape(8, 2, 2, NXD, NZD), ("tm_0", "tm_1", "tm_2", "sx", "sz")
    )
    return jax.shard_map(
        shards,
        mesh=split,
        in_specs=(
            P(TM, SPACE, None, None),
            P(SPACE, None, None),
            P(TM, SPACE, None, None),
            P(TM, SPACE, None, None),
            P(TM, SPACE),
            P(TM, SPACE),
            P(TM, SPACE, None, None),
        ),
        out_specs=(P(TM, SPACE, None, None), P(TM, SPACE, None, None)),
        check_vma=False,
    )
```

time: 605 us -> 448 us (0.74)
  waiting for transfers between devices: 422 us -> 265 us
  Pallas kernels: 0 us -> 149 us
  other arithmetic: 80.9 us -> 12.4 us
  starting transfers between devices: 36.3 us -> 0.24 us
  local copies, waits for them, and re-layouts: 36.4 us -> 6.94 us
  matrix products: 11.8 us -> 0 us
    ppermute x18 -> x0, waiting for transfers between devices: 206 us -> none  [the longest x9 132 us: extended(): lax.ppermute(head, axis, [((i + 1) % count, i) for i in range(ends)])]
    pallas_call x0 -> x1, Pallas kernels: none -> 149 us  [fine(): pl.pallas_call(fine_kernel, out_shape=jax.ShapeDtypeStruct(g.shape, jnp.f...]
    all_gather x6, waiting for transfers between devices: 215 us -> 263 us  [carried_in(): pieces = jax.tree.map(lambda part: lax.all_gather(part, axis), total)]
    ppermute x18 -> x0, starting transfers between devices: 36.1 us -> none  [the longest x9 24.5 us: extended(): lax.ppermute(tail, axis, [(i, (i + 1) % count) for i in range(ends)])]
    select_n x33 -> x0, other arithmetic: 33.2 us -> none  [the longest x24 25.3 us: advance(): jnp.where(inside, (wide_rhs + COND * beside_sum(padded_rows)) * wide_inve...]
    gather x8 -> x0, local copies, waits for them, and re-layouts: 14.2 us -> none  [interface_fix(): picked = delta[tile_rows]]
    reshape x24 -> x0, local copies, waits for them, and re-layouts: 13.5 us -> none  [the longest x8 9.57 us: interface_fix(): delta = (field - previous).reshape(-1, tile_len)]
    dot_general x8 -> x0, matrix products: 11.8 us -> none  [interface_fix(): jnp.einsum('src,sc->sr', blocks, picked, precision=lax.Precision.HIGHEST)]
  transfers between devices with their start and end apart: 24 -> 6, of which waited for: 23 -> 6; matrix products, arithmetic and copies ran while one was open for 19% -> 0% of each run, Pallas kernels for 0% -> 0%
where the time goes in v1:
time: 448 us
  waiting for transfers between devices  265 us (59%)
  Pallas kernels  149 us (33%)
  between operations  14.2 us (3%)
  other arithmetic  12.4 us (3%)
  local copies, waits for them, and re-layouts  6.94 us (2%)
    all_gather x6, waiting for transfers between devices, carried_in(): pieces = jax.tree.map(lambda part: lax.all_gather(part, axis), total)  263 us
    pallas_call x1, Pallas kernels, fine(): pl.pallas_call(fine_kernel, out_shape=jax.ShapeDtypeStruct(g.shape, jnp.f...  149 us
  transfers between devices with their start and end apart: 6, of which 6 were waited for; matrix products, arithmetic and copies ran while one was open for 0% of the time, Pallas kernels for 0%

profile of v1, /device:TPU:1, one launch (start us, length us, event | category | flops | bytes accessed | tf_op | source)
XLA Modules:
  0.0 447.8 jit_solution(15995327611387992584)
XLA Ops:
  7.2 0.7 copy.10.cnt_ref
  7.9 1.0 copy-done
  9.0 1.6 copy-done.2
  10.6 1.0 copy-done.3
  11.6 1.0 copy-done.4
  12.7 0.7 copy-done.5
  13.4 149.3 %shard_map.86 = f32[1,4,128,256]{3,2,1,0:T(8,128)S(1)} custom-call(f32[1,4,128,256]{3,2,1,0:T(8,128)S(1)} %copy-done, f32[4,128,256]{2,1,0:T(8,128)S(1)} %copy-done.3, f32[1,4,128,256]{3,2,1,0:T(8,128)S(1)} %copy-done.4, s32[8,8]{1,0:T(8,128)S(1)} %copy-done.5, s32[8,1]{1,0:T(8,128)S(1)} %copy.10.cnt_ref, f32[8,8,64,64]{3,2,1,0:T(8,128)S(1)} %copy-done.2), custom_call_target="tpu_custom_call" | custom-call | tf_op jit(solution)/shard_map/pallas_call | solution.py:368
  162.7 1.1 broadcast_select_fusion
  163.8 0.0 all-gather.13.cloned.1.call-start
  163.9 0.7 all-gather.13.cloned.1.call-update
  164.6 42.6 %all-gather.7.cloned.1.call-done = f32[2,4,128,256]{3,2,1,0:T(8,128)} async-done(((f32[1,4,128,256]{3,2,1,0:T(8,128)}), f32[2,4,128,256]{3,2,1,0:T(8,128)}) %all-gather.7.cloned.1.call-update) | async-done | bytes 1048592 | tf_op jit(solution)/shard_map/all_gather | solution.py:39
  207.2 21.2 %all-gather.13.cloned.1.call-done = f32[2,4,128,256]{3,2,1,0:T(8,128)} async-done(((f32[1,4,128,256]{3,2,1,0:T(8,128)}), f32[2,4,128,256]{3,2,1,0:T(8,128)}) %all-gather.13.cloned.1.call-update) | async-done | bytes 1048592 | tf_op jit(solution)/shard_map/all_gather | solution.py:39
  228.4 2.6 slice_multiply_fusion.1
  231.1 0.0 all-gather.15.cloned.1.call-start
  231.1 0.5 all-gather.15.cloned.1.call-update
  231.7 44.3 %all-gather.9.cloned.1.call-done = f32[2,4,128,256]{3,2,1,0:T(8,128)} async-done(((f32[1,4,128,256]{3,2,1,0:T(8,128)}), f32[2,4,128,256]{3,2,1,0:T(8,128)}) %all-gather.9.cloned.1.call-update) | async-done | bytes 1048592 | tf_op jit(solution)/shard_map/all_gather | solution.py:39
  276.0 43.9 %all-gather.15.cloned.1.call-done = f32[2,4,128,256]{3,2,1,0:T(8,128)} async-done(((f32[1,4,128,256]{3,2,1,0:T(8,128)}), f32[2,4,128,256]{3,2,1,0:T(8,128)}) %all-gather.15.cloned.1.call-update) | async-done | bytes 1048592 | tf_op jit(solution)/shard_map/all_gather | solution.py:39
  319.8 2.7 slice_multiply_fusion
  322.5 0.0 all-gather.17.cloned.1.call-start
  322.6 0.5 all-gather.17.cloned.1.call-update
  323.1 52.9 %all-gather.11.cloned.1.call-done = f32[8,4,128,256]{3,2,1,0:T(8,128)} async-done(((f32[1,4,128,256]{3,2,1,0:T(8,128)}), f32[8,4,128,256]{3,2,1,0:T(8,128)}) %all-gather.11.cloned.1.call-update) | async-done | bytes 4194320 | tf_op jit(solution)/shard_map/all_gather | solution.py:39
  376.0 58.1 %all-gather.17.cloned.1.call-done = f32[8,4,128,256]{3,2,1,0:T(8,128)} async-done(((f32[1,4,128,256]{3,2,1,0:T(8,128)}), f32[8,4,128,256]{3,2,1,0:T(8,128)}) %all-gather.17.cloned.1.call-update) | async-done | bytes 4194320 | tf_op jit(solution)/shard_map/all_gather | solution.py:39
  434.1 6.0 %fusion.3 = f32[1,4,128,256]{3,2,1,0:T(8,128)} fusion(f32[8,4,128,256]{3,2,1,0:T(8,128)} %all-gather.17.cloned.1.call-done, f32[1,4,128,256]{3,2,1,0:T(8,128)S(1)} %copy-done.7, f32[1,4,128,256]{3,2,1,0:T(8,128)} %get-tuple-element.3, f32[1,4,128,256]{3,2,1,0:T(8,128)S(1)} %copy-done.1, f32[8,4,128,256]{3,2,1,0:T(8,128)} %all-gather.11.cloned.1.call-done, ...), kind=kLoop, calls=%fused_computation.5 | loop fusion | flops 7733248 | bytes 13631500 | tf_op jit(solution)/shard_map/add | solution.py:422
  440.1 0.8 copy.12
  (21 shorter events, 0.2 us)
Async XLA Ops:
  7.2 200.1 %all-gather.7.cloned.1.call-start = ((), (), s32[]{:S(2)}) async-start(), calls=%async_computation | async-start | bytes 1572864 | tf_op jit(solution)/shard_map/all_gather | solution.py:39
  7.9 1.0 copy-start
  9.0 1.6 copy-start.2
  10.6 1.0 copy-start.3
  11.6 1.0 copy-start.4
  12.7 0.7 copy-start.5
  13.4 149.4 %copy-start.9 = (f32[1,4,128,256]{3,2,1,0:T(8,128)S(1)}, f32[1,4,128,256]{3,2,1,0:T(8,128)}, u32[]{:S(2)}) copy-start(f32[1,4,128,256]{3,2,1,0:T(8,128)} %param.10) | copy-start | bytes 1572868
  163.8 64.6 %all-gather.13.cloned.1.call-start = ((), (), s32[]{:S(2)}) async-start(), calls=%async_computation.3 | async-start | bytes 1572864 | tf_op jit(solution)/shard_map/all_gather | solution.py:39
  164.6 269.5 %copy-start.1 = (f32[1,4,128,256]{3,2,1,0:T(8,128)S(1)}, f32[1,4,128,256]{3,2,1,0:T(8,128)}, u32[]{:S(2)}) copy-start(f32[1,4,128,256]{3,2,1,0:T(8,128)} %g_ref.1) | copy-start | bytes 1572868
  164.6 111.4 %all-gather.9.cloned.1.call-start = ((), (), s32[]{:S(2)}) async-start(), calls=%async_computation.1 | async-start | bytes 1572864 | tf_op jit(solution)/shard_map/all_gather | solution.py:39
  207.2 226.8 %copy-start.8 = (f32[2,4,128,256]{3,2,1,0:T(8,128)S(1)}, f32[2,4,128,256]{3,2,1,0:T(8,128)}, u32[]{:S(2)}) copy-start(f32[2,4,128,256]{3,2,1,0:T(8,128)} %all-gather.7.cloned.1.call-done) | copy-start | bytes 3145732
  231.0 203.1 %copy-start.6 = (f32[1,4,128,256]{3,2,1,0:T(8,128)S(1)}, f32[1,4,128,256]{3,2,1,0:T(8,128)}, u32[]{:S(2)}) copy-start(f32[1,4,128,256]{3,2,1,0:T(8,128)} %get-tuple-element.4) | copy-start | bytes 1572868
  231.0 203.1 %copy-start.7 = (f32[1,4,128,256]{3,2,1,0:T(8,128)S(1)}, f32[1,4,128,256]{3,2,1,0:T(8,128)}, u32[]{:S(2)}) copy-start(f32[1,4,128,256]{3,2,1,0:T(8,128)} %get-tuple-element.5) | copy-start | bytes 1572868
  231.1 88.8 %all-gather.15.cloned.1.call-start = ((), (), s32[]{:S(2)}) async-start(), calls=%async_computation.4 | async-start | bytes 1572864 | tf_op jit(solution)/shard_map/all_gather | solution.py:39
  231.6 144.4 %all-gather.11.cloned.1.call-start = ((), (), s32[]{:S(2)}) async-start(), calls=%async_computation.2 | async-start | bytes 4718592 | tf_op jit(solution)/shard_map/all_gather | solution.py:39
  322.5 111.6 %all-gather.17.cloned.1.call-start = ((), (), s32[]{:S(2)}) async-start(), calls=%async_computation.5 | async-start | bytes 4718592 | tf_op jit(solution)/shard_map/all_gather | solution.py:39
Sparse Core Ops, SparseCore 0:
  163.9 43.2 all-gather.6
  209.9 18.4 all-gather.12
  231.2 44.7 all-gather.8
  278.5 41.3 all-gather.14
  322.7 53.3 all-gather.10
  377.9 56.0 all-gather.16

commit v2 on v1

--- a/solution.py
+++ b/solution.py
@@ -15,8 +15,10 @@
 
 NZD = 4
 NXD = 4
+NYD = 8
 DEEP = 4
 LAYERS = DEEP * NZD
+HALF = LAYERS // 2
 ROWS = 32
 NY = ROWS * NZD
 NZ = 256
@@ -25,45 +27,53 @@
 PAIRS = MAXT // 2
 
 
-def nothing_yet(x, identity):
-    return jax.tree.map(
-        lambda a, e: jnp.broadcast_to(jnp.asarray(e, a.dtype), a.shape), x, identity
-    )
-
-
-def carried_in(x, axes, combine, identity):
-    before = start = nothing_yet(x, identity)
-    total = x
-    for axis in reversed(axes):
-        length, position = (lax.axis_size(axis), lax.axis_index(axis))
-        pieces = jax.tree.map(lambda part: lax.all_gather(part, axis), total)
-        inside, total = (start, start)
-        for k in range(length):
-            passed = k < position
-            total = combine(total, jax.tree.map(lambda part: part[k], pieces))
-            inside = jax.tree.map(lambda new, old: jnp.where(passed, new, old), total, inside)
-        before = combine(inside, before)
-    return before
-
-
 def fine_kernel(
-    g_ref, c_ref, f_ref, ids_ref, cnt_ref, m_ref,
-    e_ref,
-    p, a, b, inv, cap, src, rhs, back,
+    g_ref, c_ref, f_ref, d_ref, ids_ref, cnt_ref, m_ref,
+    x_ref, e_ref,
+    p, a, b, inv, cap, src, rhs, dec, gp, back, xback,
     xlo, xhi, zlo, zhi, zs_lo, zs_hi, inv_lo, inv_hi,
-    bt, idv, dx, ids_s,
+    bt, idv, dx,
+    do, go, eo, a0, a1, ga0, ga1, ac, ao, ay, b0, bc, bo, pin, pout, x0, x1,
+    ids_s,
     in_send, in_recv, id_send, id_recv, h_send, h_recv, b_send, b_recv, o_send, o_recv, loc,
+    cs_send, cs_recv, a_send, a_recv, z_send, z_recv, y_send, y_recv, x_send, x_recv,
 ):
     sx = lax.axis_index("sx")
     sz = lax.axis_index("sz")
+    y = lax.axis_index("tm_0")
+    zh = lax.axis_index("tm_1")
+    core = lax.axis_index("tm_2")
+    dz = 1 - 2 * zh
+    q = (NZD - 1) * zh + dz * sz
+
+    def quarter(device):
+        return (NZD - 1) * zh + dz * device
+
     has_xl, has_xr = sx > 0, sx < NXD - 1
-    has_zl, has_zr = sz > 0, sz < NZD - 1
+    has_bl, has_br = sz > 0, sz < NZD - 1
+    has_zl, has_zr = q > 0, q < NZD - 1
+    has_yl, has_yr = y > 0, y < NYD - 1
+    across = {"tm_1": 1 - zh, "sz": NZD - 1 - sz}
+    beside = {"tm_2": 1 - core}
 
     barrier = pltpu.get_barrier_semaphore()
     for o in range(1, NZD):
         pl.semaphore_signal(
             barrier, inc=1, device_id={"sz": lax.rem(sz + o, NZD)}, device_id_type=MESH
         )
+    for t in range(NZD):
+        pl.semaphore_signal(
+            barrier, inc=1, device_id={"tm_2": 1 - core, "sz": t}, device_id_type=MESH
+        )
+    pl.semaphore_signal(barrier, inc=1, device_id=across, device_id_type=MESH)
+
+    @pl.when(has_yl)
+    def _():
+        pl.semaphore_signal(barrier, inc=1, device_id={"tm_0": y - 1}, device_id_type=MESH)
+
+    @pl.when(has_yr)
+    def _():
+        pl.semaphore_signal(barrier, inc=1, device_id={"tm_0": y + 1}, device_id_type=MESH)
 
     @pl.when(has_xl)
     def _():
@@ -100,15 +110,18 @@
         zhi[...] = zero_z
 
     pl.semaphore_wait(
-        barrier, NZD - 1 + has_xl.astype(jnp.int32) + has_xr.astype(jnp.int32)
+        barrier,
+        2 * NZD
+        + has_xl.astype(jnp.int32) + has_xr.astype(jnp.int32)
+        + has_yl.astype(jnp.int32) + has_yr.astype(jnp.int32),
     )
 
     def dealt(n, o):
         to = lax.rem(sz + o, NZD)
-        source = (g_ref.at[0], f_ref.at[0], c_ref)[n]
-        target = (p, src, cap)[n]
-        return pltpu.make_async_remote_copy(
-            src_ref=source.at[:, pl.ds(ROWS * to, ROWS), :],
+        source = (g_ref.at[0], f_ref.at[0], c_ref, d_ref.at[0])[n]
+        target = (p, src, cap, dec)[n]
+        return pltpu.make_async_remote_copy(
+            src_ref=source.at[:, pl.ds(ROWS * quarter(to), ROWS), :],
             dst_ref=target.at[pl.ds(DEEP * sz, DEEP)],
             send_sem=in_send.at[n, o],
             recv_sem=in_recv.at[n, o],
@@ -145,20 +158,20 @@
         )
 
     def block_start(k, r):
-        @pl.when(jnp.logical_and(sz - r >= 0, has_zr))
+        @pl.when(jnp.logical_and(sz - r >= 0, has_br))
         def _():
             block_copy(k, 0, r).start()
 
-        @pl.when(jnp.logical_and(sz + r < NZD, has_zl))
+        @pl.when(jnp.logical_and(sz + r < NZD, has_bl))
         def _():
             block_copy(k, 1, r).start()
 
     def block_wait(k, r):
-        @pl.when(jnp.logical_and(sz - r >= 0, has_zr))
+        @pl.when(jnp.logical_and(sz - r >= 0, has_br))
         def _():
             block_copy(k, 0, r).wait_send()
 
-        @pl.when(jnp.logical_and(sz + r < NZD, has_zl))
+        @pl.when(jnp.logical_and(sz + r < NZD, has_bl))
         def _():
             block_copy(k, 1, r).wait_send()
 
@@ -172,9 +185,11 @@
 
     block_start(0, 0)
     mine = pl.ds(DEEP * sz, DEEP)
-    p[mine] = g_ref[0, :, pl.ds(ROWS * sz, ROWS), :]
-    src[mine] = f_ref[0, :, pl.ds(ROWS * sz, ROWS), :]
-    cap[mine] = c_ref[:, pl.ds(ROWS * sz, ROWS), :]
+    own_rows = pl.ds(ROWS * q, ROWS)
+    p[mine] = g_ref[0, :, own_rows, :]
+    src[mine] = f_ref[0, :, own_rows, :]
+    cap[mine] = c_ref[:, own_rows, :]
+    dec[mine] = d_ref[0, :, own_rows, :]
     for o in range(1, NZD):
         listed(o).wait()
     lists = pltpu.make_async_copy(idv, ids_s, loc)
@@ -188,6 +203,7 @@
 
     for l in range(LAYERS):
         inv[l] = 1.0 / (cap[l] + 6.0 * COND)
+        gp[l] = p[l]
     inv_lo[...] = inv[:, 0, :]
     inv_hi[...] = inv[:, ROWS - 1, :]
     zs_lo[0] = p[:, 0, :]
@@ -208,7 +224,8 @@
             )
 
         xl, xr = {"sx": jnp.maximum(sx - 1, 0)}, {"sx": jnp.minimum(sx + 1, NXD - 1)}
-        zl, zr = {"sz": jnp.maximum(sz - 1, 0)}, {"sz": jnp.minimum(sz + 1, NZD - 1)}
+        zl = {"sz": jnp.clip(sz - dz, 0, NZD - 1)}
+        zr = {"sz": jnp.clip(sz + dz, 0, NZD - 1)}
         return (
             (has_xl, has_xr, lambda: copy(0, field.at[0], xhi.at[slot], xl)),
             (has_xr, has_xl, lambda: copy(1, field.at[LAYERS - 1], xlo.at[slot], xr)),
@@ -273,7 +290,7 @@
                     slot = 2 * i + odd
                     tile = ids_s[brick, k, slot]
                     quad = lax.rem(tile, 4)
-                    line = lax.rem(tile // 4, NY) - ROWS * sz
+                    line = lax.rem(tile // 4, NY) - ROWS * q
                     layer = tile // (4 * NY)
                     owned = (line >= 0) & (line < ROWS) & (slot < count)
                     line_in = jnp.clip(line, 0, ROWS - 1)
@@ -313,10 +330,98 @@
 
     dx[...] = jnp.zeros((128, 128), jnp.float32)
 
+    half = pl.ds(HALF * core, HALF)
+    rest = pl.ds(HALF * (1 - core), HALF)
+    first_slab = jnp.logical_and(y == 0, zh == 0)
+
+    def swapped(n, source, target):
+        return pltpu.make_async_remote_copy(
+            src_ref=source.at[rest],
+            dst_ref=target,
+            send_sem=cs_send.at[n],
+            recv_sem=cs_recv.at[n],
+            device_id=beside,
+            device_id_type=MESH,
+        )
+
+    def factors(n):
+        return swapped(n, (dec, gp)[n], (do, go)[n])
+
+    def factors_ready():
+        for i in range(HALF):
+            own_d, own_g = dec[HALF * core + i], gp[HALF * core + i]
+            d0 = jnp.where(core == 0, own_d, do[i])
+            d1 = jnp.where(core == 0, do[i], own_d)
+            g0 = jnp.where(core == 0, own_g, go[i])
+            g1 = jnp.where(core == 0, go[i], own_g)
+            d0 = jnp.where(first_slab, 0.0, d0)
+            a0[i] = d0
+            a1[i] = d1
+            ga0[i] = d0 * g0
+            ga1[i] = d1 * g1
+            ac[i] = d0 * d1
+            pout[i] = g0
+
+    def scales():
+        return pltpu.make_async_remote_copy(
+            src_ref=ac,
+            dst_ref=ao,
+            send_sem=a_send,
+            recv_sem=a_recv,
+            device_id=across,
+            device_id_type=MESH,
+        )
+
+    def shift(i):
+        return pltpu.make_async_remote_copy(
+            src_ref=bc.at[i],
+            dst_ref=bo.at[i],
+            send_sem=z_send.at[i],
+            recv_sem=z_recv.at[i],
+            device_id=across,
+            device_id_type=MESH,
+        )
+
+    def state(i):
+        return pltpu.make_async_remote_copy(
+            src_ref=pout.at[i],
+            dst_ref=pin.at[i],
+            send_sem=y_send.at[i],
+            recv_sem=y_recv.at[i],
+            device_id={"tm_0": jnp.minimum(y + 1, NYD - 1)},
+            device_id_type=MESH,
+        )
+
     def step(k, carry):
         def one():
             block_wait(k, 1)
             block_start(k, 2)
+
+        def two():
+            for o in range(1, NZD):
+                @pl.when(k == o - 1)
+                def _(o=o):
+                    dealt(3, o).start()
+
+            @pl.when(k == 3)
+            def _():
+                for o in range(1, NZD):
+                    dealt(3, o).wait()
+                factors(0).start()
+                factors(1).start()
+
+            @pl.when(k == 4)
+            def _():
+                factors(0).wait()
+                factors(1).wait()
+                factors_ready()
+                scales().start()
+
+            @pl.when(k == 5)
+            def _():
+                scales().wait()
+                for i in range(HALF):
+                    ay[i] = ac[i] * ao[i]
 
         def three():
             @pl.when(k < INCREMENTS - 1)
@@ -330,7 +435,7 @@
                 block_start(k + 1, 1)
 
         sweep(p, a, 0, True, False, one)
-        sweep(a, b, 1, False, False, lambda: None)
+        sweep(a, b, 1, False, False, two)
         sweep(b, a, 0, False, False, three)
         sweep(a, b, 1, False, True, four)
         block_wait(k, 2)
@@ -343,84 +448,131 @@
         to = lax.rem(sz + o, NZD)
         return pltpu.make_async_remote_copy(
             src_ref=p.at[pl.ds(DEEP * to, DEEP)],
-            dst_ref=back.at[:, pl.ds(ROWS * sz, ROWS), :],
+            dst_ref=back.at[:, own_rows, :],
             send_sem=o_send.at[o],
             recv_sem=o_recv.at[o],
             device_id={"sz": to},
             device_id_type=MESH,
         )
 
+    swapped(2, p, eo).start()
+    swapped(2, p, eo).wait()
+    for i in range(HALF):
+        own = p[HALF * core + i]
+        s0 = jnp.where(core == 0, own, eo[i]) - ga0[i]
+        s1 = jnp.where(core == 0, eo[i], own) - ga1[i]
+        b0[i] = s0
+        bc[i] = a1[i] * s0 + s1
+        shift(i).start()
     for o in range(1, NZD):
         returned(o).start()
-    back[:, pl.ds(ROWS * sz, ROWS), :] = p[mine]
+    back[:, own_rows, :] = p[mine]
+
+    def sent(slab, part, source):
+        return pltpu.make_async_remote_copy(
+            src_ref=(x0, x1)[slab].at[pl.ds(DEEP * part, DEEP)],
+            dst_ref=xback.at[:, pl.ds(ROWS * quarter(source), ROWS), :],
+            send_sem=x_send.at[slab, part],
+            recv_sem=x_recv.at[source],
+            device_id={"tm_2": slab, "sz": 2 * core + part},
+            device_id_type=MESH,
+        )
+
+    def stays(slab, part):
+        return jnp.logical_and(core == slab, sz == 2 * core + part)
+
+    for i in range(HALF):
+        shift(i).wait()
+
+        @pl.when(has_yl)
+        def _(i=i):
+            state(i).wait_recv()
+            before = pin[i]
+            pout[i] = before
+
+        before = pout[i]
+        shift_0 = jnp.where(zh == 0, bc[i], bo[i])
+        shift_1 = jnp.where(zh == 0, bo[i], bc[i])
+        scale_0 = jnp.where(zh == 0, ac[i], ao[i])
+        scale_1 = jnp.where(zh == 0, ao[i], ac[i])
+        pout[i] = ay[i] * before + (scale_1 * shift_0 + shift_1)
+
+        @pl.when(has_yr)
+        def _(i=i):
+            state(i).start()
+
+        start = jnp.where(zh == 0, before, scale_0 * before + shift_0)
+        x0[i] = start
+        x1[i] = a0[i] * start + b0[i]
+        if i % DEEP == DEEP - 1:
+            part = i // DEEP
+            for slab in range(2):
+                @pl.when(jnp.logical_not(stays(slab, part)))
+                def _(slab=slab, part=part):
+                    sent(slab, part, sz).start()
+
+                @pl.when(stays(slab, part))
+                def _(slab=slab, part=part):
+                    xback[:, own_rows, :] = (x0, x1)[slab][DEEP * part : DEEP * (part + 1)]
+
     for o in range(1, NZD):
         returned(o).wait()
     e_ref[0] = back[...]
-
-
-def fine(g, c, f, ids, cnt, m):
+    for slab in range(2):
+        for part in range(2):
+            @pl.when(jnp.logical_not(stays(slab, part)))
+            def _(slab=slab, part=part):
+                sent(slab, part, sz).wait_send()
+
+    for t in range(NZD):
+        @pl.when(jnp.logical_not(jnp.logical_and(core == sz // 2, sz == t)))
+        def _(t=t):
+            sent(0, 0, t).wait_recv()
+
+    for i in range(HALF):
+        @pl.when(has_yr)
+        def _(i=i):
+            state(i).wait_send()
+
+    x_ref[0] = xback[...]
+
+
+def shards(g, c, f, d, ids, cnt, m):
     vm = pl.BlockSpec(memory_space=pltpu.VMEM)
     field = pltpu.VMEM((LAYERS, ROWS, NZ), jnp.float32)
+    brick = pltpu.VMEM((DEEP, NY, NZ), jnp.float32)
+    part = pltpu.VMEM((HALF, ROWS, NZ), jnp.float32)
     xf = pltpu.VMEM((2, ROWS, NZ), jnp.float32)
     zf = pltpu.VMEM((2, LAYERS, NZ), jnp.float32)
     z1 = pltpu.VMEM((LAYERS, NZ), jnp.float32)
     dma = pltpu.SemaphoreType.DMA
+    out = jax.ShapeDtypeStruct(g.shape, jnp.float32)
     return pl.pallas_call(
         fine_kernel,
-        out_shape=jax.ShapeDtypeStruct(g.shape, jnp.float32),
-        in_specs=[vm] * 6,
-        out_specs=vm,
-        scratch_shapes=[field] * 7
-        + [pltpu.VMEM((DEEP, NY, NZ), jnp.float32)]
+        out_shape=(out, out),
+        in_specs=[vm] * 7,
+        out_specs=(vm, vm),
+        scratch_shapes=[field] * 9
+        + [brick] * 2
         + [xf, xf, zf, zf, zf, zf, z1, z1]
         + [
             pltpu.VMEM((INCREMENTS, NZD, PAIRS, TILE, 128), jnp.float32),
             pltpu.VMEM((NZD, INCREMENTS, 128), jnp.int32),
             pltpu.VMEM((128, 128), jnp.float32),
+        ]
+        + [part] * 17
+        + [
             pltpu.SMEM((NZD, INCREMENTS, 128), jnp.int32),
-            dma((3, NZD)), dma((3, NZD)), dma((NZD,)), dma((NZD,)),
+            dma((4, NZD)), dma((4, NZD)), dma((NZD,)), dma((NZD,)),
             dma((4, 2)), dma((4, 2)), dma((2, 2, 3)), dma((2, 2, 3)),
             dma((NZD,)), dma((NZD,)), dma,
+            dma((3,)), dma((3,)), dma, dma, dma((HALF,)), dma((HALF,)),
+            dma((HALF,)), dma((HALF,)), dma((2, 2)), dma((NZD,)),
         ],
         compiler_params=pltpu.CompilerParams(
             collective_id=0, has_side_effects=True, vmem_limit_bytes=48 << 20
         ),
-    )(g, c, f, ids, cnt, m)
-
-
-def shards(
-    opening_guess_profile,
-    capacity,
-    thermal_forcing,
-    rough_decay_factor,
-    tile_ids,
-    tile_count,
-    tile_blocks,
-):
-    opening_moment = opening_guess_profile[0]
-    rough_estimate = rough_decay_factor[0]
-    accurate_ending_thermal_state = fine(
-        opening_guess_profile, capacity, thermal_forcing, tile_ids, tile_count, tile_blocks
-    )[0]
-    opening_window = lax.axis_index(TM) == 0
-    own_scale = jnp.where(opening_window, 0.0, rough_estimate)
-    own_shift = jnp.where(
-        opening_window,
-        accurate_ending_thermal_state,
-        accurate_ending_thermal_state - rough_estimate * opening_moment,
-    )
-
-    def compose(prior_iterate, later):
-        return (later[0] * prior_iterate[0], later[0] * prior_iterate[1] + later[1])
-
-    scale, shift = carried_in(
-        (own_scale, own_shift),
-        TM,
-        compose,
-        (jnp.ones_like(rough_estimate), jnp.zeros_like(rough_estimate)),
-    )
-    updated_opening_state = scale * opening_moment + shift
-    return (updated_opening_state[None], accurate_ending_thermal_state[None])
+    )(g, c, f, d, ids, cnt, m)
 
 
 def solution(mesh):

time: 448 us -> 229 us (0.51)
  the two profiles are of different devices: /device:TPU:1 before, /device:TPU:121 now
where the time goes in v2:
time: 229 us
  Pallas kernels  219 us (96%)
  local copies, waits for them, and re-layouts  8.76 us (4%)
    pallas_call x1, Pallas kernels, shards(): pl.pallas_call(fine_kernel, out_shape=(out, out), in_specs=[vm] * 7, out_...  219 us
    unnamed x15, local copies, waits for them, and re-layouts  8.76 us

profile of v2, /device:TPU:121, one launch (start us, length us, event | category | flops | bytes accessed | tf_op | source)
XLA Modules:
  0.0 228.7 jit_solution(10673607765681595992)
XLA Ops:
  0.6 0.7 copy.9.cnt_ref
  1.4 0.0 copy-start
  1.4 1.6 copy-done
  3.0 0.0 copy-start.1
  3.0 1.0 copy-done.1
  4.0 0.0 copy-start.2
  4.0 1.0 copy-done.2
  5.0 0.0 copy-start.3
  5.0 1.0 copy-done.3
  6.1 0.0 copy-start.4
  6.1 1.0 copy-done.4
  7.1 0.0 copy-start.5
  7.1 0.7 copy-done.5
  7.8 219.3 %shard_map.86 = (f32[1,4,128,256]{3,2,1,0:T(8,128)S(1)}, f32[1,4,128,256]{3,2,1,0:T(8,128)S(1)}) custom-call(f32[1,4,128,256]{3,2,1,0:T(8,128)S(1)} %copy-done.1, f32[4,128,256]{2,1,0:T(8,128)S(1)} %copy-done.2, f32[1,4,128,256]{3,2,1,0:T(8,128)S(1)} %copy-done.3, f32[1,4,128,256]{3,2,1,0:T(8,128)S(1)} %copy-done.4, s32[8,8]{1,0:T(8,128)S(1)} %copy-done.5, ...), custom_call_target="tpu_custom_call" | custom-call | tf_op jit(solution)/shard_map/pallas_call | solution.py:550
  227.1 0.8 copy.12
  227.9 0.8 copy.13
Async XLA Ops:
  1.4 1.6 copy-start
  3.0 1.0 copy-start.1
  4.0 1.0 copy-start.2
  5.0 1.0 copy-start.3
  6.1 1.0 copy-start.4
  7.1 0.7 copy-start.5

commit v3 on v2

v3 whole, which is shorter than its diff:
```python
import jax
import jax.numpy as jnp
from jax import lax
from jax.experimental import pallas as pl
from jax.experimental.pallas import tpu as pltpu
from jax.sharding import Mesh
from jax.sharding import PartitionSpec as P

INCREMENTS = 8
SWEEPS = 4
TM = ("tm_0", "tm_1", "tm_2")
SPACE = ("sx", "sz")
MESH = pl.DeviceIdType.MESH
COND = 1.0

NZD = 4
NXD = 4
NYD = 8
DEEP = 4
LAYERS = DEEP * NZD
HALF = LAYERS // 2
ROWS = 32
NY = ROWS * NZD
NZ = 256
TILE = 64
MAXT = 8
PAIRS = MAXT // 2
LAST = 2 * INCREMENTS - 2


def kernel(
    g_ref, c_ref, f_ref, d_ref, ids_ref, cnt_ref, m_ref,
    x_ref, e_ref,
    p, a, b, inv, cap, src, rhs, dec, gp, back, xback,
    xlo, xhi, zlo, zhi, zs_lo, zs_hi, corner,
    inv_lo, inv_hi, cz_lo, cz_hi, fz_lo, fz_hi,
    rc_xl, rc_xh, rc_zl, rc_zh, rf_xl, rf_xh, rf_zl, rf_zh,
    rr_xl, rr_xh, rr_zl, rr_zh, w_xl, w_xh, w_zl, w_zh,
    mv, ids_v, cnt_v, bt, idv, dx,
    do, go, eo, a0, a1, ga0, ga1, ac, ao, ay, b0, bc, bo, pin, pout, x0, x1,
    ids_s,
    in_send, in_recv, c_send, c_recv, id_send, id_recv, h_send, h_recv, r_send, r_recv,
    b_send, b_recv, o_send, o_recv, loc,
    cs_send, cs_recv, s_send, s_recv, a_send, a_recv, z_send, z_recv, y_send, y_recv,
    x_send, x_recv,
):
    sx = lax.axis_index("sx")
    sz = lax.axis_index("sz")
    y = lax.axis_index("tm_0")
    zh = lax.axis_index("tm_1")
    core = lax.axis_index("tm_2")
    dz = 1 - 2 * zh
    q = (NZD - 1) * zh + dz * sz
    ring = NZD * zh + sz

    def quarter(device):
        return (NZD - 1) * zh + dz * device

    has_xl, has_xr = sx > 0, sx < NXD - 1
    has_bl, has_br = sz > 0, sz < NZD - 1
    has_zl, has_zr = q > 0, q < NZD - 1
    has_yl, has_yr = y > 0, y < NYD - 1
    across = {"tm_1": 1 - zh, "sz": NZD - 1 - sz}
    beside = {"tm_2": 1 - core}
    xl_at, xr_at = jnp.maximum(sx - 1, 0), jnp.minimum(sx + 1, NXD - 1)
    zl_at, zr_at = jnp.clip(sz - dz, 0, NZD - 1), jnp.clip(sz + dz, 0, NZD - 1)
    sides = (
        (has_xl, {"sx": xl_at}),
        (has_xr, {"sx": xr_at}),
        (jnp.logical_and(has_xl, has_zl), {"sx": xl_at, "sz": zl_at}),
        (jnp.logical_and(has_xl, has_zr), {"sx": xl_at, "sz": zr_at}),
        (jnp.logical_and(has_xr, has_zl), {"sx": xr_at, "sz": zl_at}),
        (jnp.logical_and(has_xr, has_zr), {"sx": xr_at, "sz": zr_at}),
        (has_yl, {"tm_0": jnp.maximum(y - 1, 0)}),
        (has_yr, {"tm_0": jnp.minimum(y + 1, NYD - 1)}),
    )

    barrier = pltpu.get_barrier_semaphore()
    expected = jnp.int32(4 * NZD - 1)
    for other in range(1, 4 * NZD):
        place = lax.rem(4 * NZD + 2 * ring + core - other, 4 * NZD)
        pl.semaphore_signal(
            barrier,
            inc=1,
            device_id={
                "tm_2": lax.rem(place, 2),
                "tm_1": place // (2 * NZD),
                "sz": lax.rem(place // 2, NZD),
            },
            device_id_type=MESH,
        )
    for there, where in sides:
        expected = expected + there.astype(jnp.int32)

        @pl.when(there)
        def _(where=where):
            pl.semaphore_signal(barrier, inc=1, device_id=where, device_id_type=MESH)

    own_rows = pl.ds(ROWS * q, ROWS)
    mine = pl.ds(DEEP * sz, DEEP)
    local = [
        pltpu.make_async_copy(ids_ref, ids_v, loc.at[0]),
        pltpu.make_async_copy(cnt_ref, cnt_v, loc.at[1]),
        pltpu.make_async_copy(m_ref, mv, loc.at[2]),
        pltpu.make_async_copy(g_ref.at[0, :, own_rows, :], p.at[mine], loc.at[3]),
        pltpu.make_async_copy(f_ref.at[0, :, own_rows, :], src.at[mine], loc.at[4]),
        pltpu.make_async_copy(c_ref.at[:, own_rows, :], cap.at[mine], loc.at[5]),
        pltpu.make_async_copy(d_ref.at[0, :, own_rows, :], dec.at[mine], loc.at[6]),
    ]
    for copy in local:
        copy.start()
    local[0].wait()
    local[1].wait()
    idv[sz] = jnp.zeros((2 * INCREMENTS, 128), jnp.int32)
    idv[sz, 0:INCREMENTS, 0:MAXT] = ids_v[...]
    idv[sz, INCREMENTS : INCREMENTS + 1, 0:INCREMENTS] = cnt_v[...]
    pl.semaphore_wait(barrier, expected)

    def dealt(n, o):
        to = lax.rem(sz + o, NZD)
        source = (g_ref.at[0], f_ref.at[0], d_ref.at[0])[n]
        target = (p, src, dec)[n]
        return pltpu.make_async_remote_copy(
            src_ref=source.at[:, pl.ds(ROWS * quarter(to), ROWS), :],
            dst_ref=target.at[mine],
            send_sem=in_send.at[n, o],
            recv_sem=in_recv.at[n, o],
            device_id={"sz": to},
            device_id_type=MESH,
        )

    steps = (1, -1, 2 - 4 * core)

    def capacity_in(n):
        to = lax.rem(ring + steps[n] + 2 * NZD, 2 * NZD)
        to_zh, to_sz = to // NZD, lax.rem(to, NZD)
        to_q = (NZD - 1) * to_zh + (1 - 2 * to_zh) * to_sz
        return pltpu.make_async_remote_copy(
            src_ref=c_ref.at[pl.ds(2 * core, 2), pl.ds(ROWS * to_q, ROWS), :],
            dst_ref=cap.at[pl.ds(DEEP * sz + 2 * core, 2)],
            send_sem=c_send.at[0, n],
            recv_sem=c_recv.at[0, n],
            device_id={"tm_1": to_zh, "sz": to_sz},
            device_id_type=MESH,
        )

    def capacity_on(n):
        origin = lax.rem(ring - steps[n] + 2 * NZD, NZD)
        part = cap.at[pl.ds(DEEP * origin + 2 * core, 2)]
        return pltpu.make_async_remote_copy(
            src_ref=part,
            dst_ref=part,
            send_sem=c_send.at[1, n],
            recv_sem=c_recv.at[1, n],
            device_id=beside,
            device_id_type=MESH,
        )

    def listed(o):
        to = lax.rem(sz + o, NZD)
        return pltpu.make_async_remote_copy(
            src_ref=idv.at[sz],
            dst_ref=idv.at[sz],
            send_sem=id_send.at[o],
            recv_sem=id_recv.at[o],
            device_id={"sz": to},
            device_id_type=MESH,
        )

    for n in range(3):
        capacity_in(n).start()
    for n in range(2):
        for o in range(1, NZD):
            dealt(n, o).start()
    for o in range(1, NZD):
        listed(o).start()

    def block_copy(n, d, r):
        brick = jnp.clip(sz - r if d == 0 else sz + r, 0, NZD - 1)
        part = bt.at[n // 2, brick, pl.ds(2 * lax.rem(n, 2), 2)]
        return pltpu.make_async_remote_copy(
            src_ref=part,
            dst_ref=part,
            send_sem=b_send.at[lax.rem(n, 4), d, r],
            recv_sem=b_recv.at[lax.rem(n, 4), d, r],
            device_id={"sz": jnp.clip(sz + 1 if d == 0 else sz - 1, 0, NZD - 1)},
            device_id_type=MESH,
        )

    def block_start(n, r):
        @pl.when(jnp.logical_and(sz - r >= 0, has_br))
        def _():
            block_copy(n, 0, r).start()

        @pl.when(jnp.logical_and(sz + r < NZD, has_bl))
        def _():
            block_copy(n, 1, r).start()

    def block_wait(n, r):
        @pl.when(jnp.logical_and(sz - r >= 0, has_br))
        def _():
            block_copy(n, 0, r).wait_send()

        @pl.when(jnp.logical_and(sz + r < NZD, has_bl))
        def _():
            block_copy(n, 1, r).wait_send()

        @pl.when(sz - 1 - r >= 0)
        def _():
            block_copy(n, 0, r).wait_recv()

        @pl.when(sz + 1 + r < NZD)
        def _():
            block_copy(n, 1, r).wait_recv()

    local[2].wait()

    def turned(k, carry):
        for i in range(PAIRS):
            two = mv[k, 2 * i : 2 * i + 2].reshape(2 * TILE, TILE)
            bt[k, sz, i] = two.T
        return carry

    lax.fori_loop(0, INCREMENTS, turned, 0)
    block_start(0, 0)
    block_start(1, 0)
    for ref, have in ((xlo, has_xl), (xhi, has_xr), (zlo, has_zl), (zhi, has_zr)):
        @pl.when(jnp.logical_not(have))
        def _(ref=ref):
            ref[...] = jnp.zeros(ref.shape, jnp.float32)

    for refs, have in (
        ((rc_xl, rf_xl), has_xl),
        ((rc_xh, rf_xh), has_xr),
        ((rc_zl, rf_zl), has_zl),
        ((rc_zh, rf_zh), has_zr),
    ):
        @pl.when(jnp.logical_not(have))
        def _(refs=refs):
            for ref in refs:
                ref[...] = jnp.zeros(ref.shape, jnp.float32)

    for n in range(4):
        @pl.when(jnp.logical_not(sides[2 + n][0]))
        def _(n=n):
            for slot in range(2):
                corner[slot, n] = jnp.zeros((8, NZ), jnp.float32)

    dx[...] = jnp.zeros((128, 128), jnp.float32)
    for copy in local[3:]:
        copy.wait()
    for n in range(3):
        capacity_in(n).wait()
    for n in range(3):
        capacity_on(n).start()
    for n in range(3):
        capacity_on(n).wait()

    def inverses(l, carry):
        inv[l] = 1.0 / (cap[l] + 6.0 * COND)
        return carry

    lax.fori_loop(0, LAYERS, inverses, 0)
    inv_lo[...] = inv[:, 0, :]
    inv_hi[...] = inv[:, ROWS - 1, :]
    cz_lo[...] = cap[:, 0, :]
    cz_hi[...] = cap[:, ROWS - 1, :]
    for n in range(2):
        for o in range(1, NZD):
            dealt(n, o).wait()
    for o in range(1, NZD):
        listed(o).wait()
    lists = pltpu.make_async_copy(idv, ids_s, loc.at[0])
    lists.start()
    fz_lo[...] = src[:, 0, :]
    fz_hi[...] = src[:, ROWS - 1, :]

    def faces(slot):
        zs_lo[slot, 0] = p[:, 0, :]
        zs_lo[slot, 1] = p[:, 1, :]
        zs_hi[slot, 0] = p[:, ROWS - 1, :]
        zs_hi[slot, 1] = p[:, ROWS - 2, :]

    faces(0)

    def moved(source, target, sems, where):
        return pltpu.make_async_remote_copy(
            src_ref=source,
            dst_ref=target,
            send_sem=sems[0],
            recv_sem=sems[1],
            device_id=where,
            device_id_type=MESH,
        )

    to_xl, to_xr = {"sx": xl_at}, {"sx": xr_at}
    to_zl, to_zr = {"sz": zl_at}, {"sz": zr_at}

    def rims():
        out = []
        for n, (field, lo, hi, xl, xh, zl, zh_) in enumerate((
            (cap, cz_lo, cz_hi, rc_xl, rc_xh, rc_zl, rc_zh),
            (src, fz_lo, fz_hi, rf_xl, rf_xh, rf_zl, rf_zh),
        )):
            for m, (sends, gets, source, target, where) in enumerate((
                (has_xl, has_xr, field.at[0], xh, to_xl),
                (has_xr, has_xl, field.at[LAYERS - 1], xl, to_xr),
                (has_zl, has_zr, lo, zh_, to_zl),
                (has_zr, has_zl, hi, zl, to_zr),
            )):
                sems = (r_send.at[n, m], r_recv.at[n, m])
                out.append((sends, gets, moved(source, target, sems, where)))
        return out

    def begin(copies):
        for sends, unused, copy in copies:
            @pl.when(sends)
            def _(copy=copy):
                copy.start()

    def end(copies):
        for sends, gets, copy in copies:
            @pl.when(gets)
            def _(copy=copy):
                copy.wait_recv()

            @pl.when(sends)
            def _(copy=copy):
                copy.wait_send()

    def halo(field, slot):
        def sems(n):
            return h_send.at[n, slot], h_recv.at[n, slot]

        ll, lh, hl, hh = sides[2][0], sides[3][0], sides[4][0], sides[5][0]
        at = [side[1] for side in sides[2:6]]
        top, low = pl.ds(0, 8), pl.ds(ROWS - 8, 8)
        last = LAYERS - 1
        return [
            (has_xl, has_xr, moved(field.at[pl.ds(0, 2)], xhi.at[slot], sems(0), to_xl)),
            (has_xr, has_xl, moved(field.at[pl.ds(last - 1, 2)], xlo.at[slot], sems(1), to_xr)),
            (has_zl, has_zr, moved(zs_lo.at[slot], zhi.at[slot], sems(2), to_zl)),
            (has_zr, has_zl, moved(zs_hi.at[slot], zlo.at[slot], sems(3), to_zr)),
            (ll, hh, moved(field.at[0, top], corner.at[slot, 3], sems(4), at[0])),
            (lh, hl, moved(field.at[0, low], corner.at[slot, 2], sems(5), at[1])),
            (hl, lh, moved(field.at[last, top], corner.at[slot, 1], sems(6), at[2])),
            (hh, ll, moved(field.at[last, low], corner.at[slot, 0], sems(7), at[3])),
        ]

    row = lax.broadcasted_iota(jnp.int32, (ROWS, NZ), 0)
    lane = lax.broadcasted_iota(jnp.int32, (ROWS, NZ), 1)
    layer_of = lax.broadcasted_iota(jnp.int32, (LAYERS, NZ), 0)
    lane_z = lax.broadcasted_iota(jnp.int32, (LAYERS, NZ), 1)

    def along(w, index):
        left = jnp.where(index == 0, 0.0, pltpu.roll(w, 1, 1))
        return left + jnp.where(index == NZ - 1, 0.0, pltpu.roll(w, NZ - 1, 1))

    def between(w, index, before, after):
        n = w.shape[0]
        up = jnp.where(index == 0, before, pltpu.roll(w, 1, 0))
        return up + jnp.where(index == n - 1, after, pltpu.roll(w, n - 1, 0))

    def inner(old, new, first):
        for l in range(LAYERS):
            w = old[l]
            t = between(w, row, 0.0, 0.0) + along(w, lane)
            if l > 0:
                t = t + old[l - 1]
            if l < LAYERS - 1:
                t = t + old[l + 1]
            if first:
                r = cap[l] * w + src[l]
                rhs[l] = r
            else:
                r = rhs[l]
            new[l] = (r + COND * t) * inv[l]

    def outer(new, xl, xh, zl, zh_):
        new[0] = new[0] + COND * (inv[0] * xl)
        new[LAYERS - 1] = new[LAYERS - 1] + COND * (inv[LAYERS - 1] * xh)
        lo = new[:, 0, :] + COND * (inv_lo[...] * zl)
        hi = new[:, ROWS - 1, :] + COND * (inv_hi[...] * zh_)
        new[:, 0, :] = lo
        new[:, ROWS - 1, :] = hi
        return lo, hi

    def inverse(c, have):
        return jnp.where(have, 1.0 / (c + 6.0 * COND), 0.0)

    def two_sweeps(old, mid, new, slot, first, early, late):
        copies = halo(old, slot)
        begin(copies)
        early()
        inner(old, mid, first)
        end(copies)
        late()
        xl, xh, zl, zh_ = xlo[slot, 1], xhi[slot, 0], zlo[slot, 0], zhi[slot, 0]
        outer(mid, xl, xh, zl, zh_)
        if first:
            rr_xl[...] = rc_xl[...] * xl + rf_xl[...]
            rr_xh[...] = rc_xh[...] * xh + rf_xh[...]
            rr_zl[...] = rc_zl[...] * zl + rf_zl[...]
            rr_zh[...] = rc_zh[...] * zh_ + rf_zh[...]
        ll, lh = corner[slot, 0, 7:8, :], corner[slot, 1, 0:1, :]
        hl, hh = corner[slot, 2, 7:8, :], corner[slot, 3, 0:1, :]
        t = xlo[slot, 0] + old[0] + between(xl, row, ll, lh) + along(xl, lane)
        w_xl[...] = (rr_xl[...] + COND * t) * inverse(rc_xl[...], has_xl)
        t = xhi[slot, 1] + old[LAYERS - 1] + between(xh, row, hl, hh) + along(xh, lane)
        w_xh[...] = (rr_xh[...] + COND * t) * inverse(rc_xh[...], has_xr)
        t = zlo[slot, 1] + zs_lo[slot, 0] + between(zl, layer_of, ll, hl) + along(zl, lane_z)
        w_zl[...] = (rr_zl[...] + COND * t) * inverse(rc_zl[...], has_zl)
        t = zhi[slot, 1] + zs_hi[slot, 0] + between(zh_, layer_of, lh, hh) + along(zh_, lane_z)
        w_zh[...] = (rr_zh[...] + COND * t) * inverse(rc_zh[...], has_zr)
        inner(mid, new, False)
        lo, hi = outer(new, w_xl[...], w_xh[...], w_zl[...], w_zh[...])
        if first:
            zs_lo[1 - slot, 0] = lo
            zs_hi[1 - slot, 0] = hi
            zs_lo[1 - slot, 1] = new[:, 1, :]
            zs_hi[1 - slot, 1] = new[:, ROWS - 2, :]

    lane_r = lax.broadcasted_iota(jnp.int32, (1, 128), 1) < TILE
    lane_c = lax.broadcasted_iota(jnp.int32, (TILE, 128), 1) < TILE
    cell = lax.broadcasted_iota(jnp.int32, (DEEP * ROWS, NZ), 0)

    def fix(k):
        places = []
        for brick in range(NZD):
            count = ids_s[brick, INCREMENTS, k]
            for i in range(PAIRS):
                halves = []
                for odd in range(2):
                    slot = 2 * i + odd
                    tile = ids_s[brick, k, slot]
                    quad = lax.rem(tile, 4)
                    line = lax.rem(tile // 4, NY) - ROWS * q
                    layer = tile // (4 * NY)
                    owned = (line >= 0) & (line < ROWS) & (slot < count)
                    line_in = jnp.clip(line, 0, ROWS - 1)
                    where = DEEP * brick + layer
                    d = b[where, pl.ds(line_in, 1), :] - p[where, pl.ds(line_in, 1), :]
                    h = jnp.where(quad >= 2, d[:, 128:], d[:, :128])
                    turn = lax.rem(quad, 2) != odd
                    h = jnp.where(turn, pltpu.roll(h, TILE, 1), h)
                    halves.append(h)
                    places.append((jnp.where(owned, layer * ROWS + line_in, -1), quad, turn))
                dx[brick * PAIRS + i : brick * PAIRS + i + 1, :] = jnp.where(
                    lane_r, halves[0], halves[1]
                )
        columns = dx[...].T
        for brick in range(NZD):
            total = b[DEEP * brick : DEEP * (brick + 1)].reshape(DEEP * ROWS, NZ)
            for i in range(PAIRS):
                at = brick * PAIRS + i
                d = jnp.where(
                    lane_c,
                    jnp.broadcast_to(columns[0:TILE, at : at + 1], (TILE, 128)),
                    jnp.broadcast_to(columns[TILE : 2 * TILE, at : at + 1], (TILE, 128)),
                )
                sums = jnp.sum(bt[k, brick, i] * d, axis=0, keepdims=True)
                for odd in range(2):
                    place, quad, turn = places[brick * MAXT + 2 * i + odd]
                    h = jnp.where(turn, pltpu.roll(sums, TILE, 1), sums)
                    right = lax.rem(quad, 2) == 1
                    h = jnp.where(lane_r != right, h, 0.0)
                    wide = jnp.concatenate(
                        [jnp.where(quad < 2, h, 0.0), jnp.where(quad < 2, 0.0, h)], axis=1
                    )
                    total = total + jnp.where(cell == place, wide, 0.0)
            p[DEEP * brick : DEEP * (brick + 1)] = total.reshape(DEEP, ROWS, NZ)
        faces(0)

    half = pl.ds(HALF * core, HALF)
    rest = pl.ds(HALF * (1 - core), HALF)
    first_slab = jnp.logical_and(y == 0, zh == 0)

    def swapped(n, source, target):
        return pltpu.make_async_remote_copy(
            src_ref=source.at[rest],
            dst_ref=target,
            send_sem=cs_send.at[n],
            recv_sem=cs_recv.at[n],
            device_id=beside,
            device_id_type=MESH,
        )

    def factors(n):
        return swapped(n, (dec, gp)[n], (do, go)[n])

    def factors_ready():
        for i in range(HALF):
            own_d, own_g = dec[HALF * core + i], gp[HALF * core + i]
            d0 = jnp.where(core == 0, own_d, do[i])
            d1 = jnp.where(core == 0, do[i], own_d)
            g0 = jnp.where(core == 0, own_g, go[i])
            g1 = jnp.where(core == 0, go[i], own_g)
            d0 = jnp.where(first_slab, 0.0, d0)
            a0[i] = d0
            a1[i] = d1
            ga0[i] = d0 * g0
            ga1[i] = d1 * g1
            ac[i] = d0 * d1
            pout[i] = g0

    def scales():
        return pltpu.make_async_remote_copy(
            src_ref=ac,
            dst_ref=ao,
            send_sem=a_send,
            recv_sem=a_recv,
            device_id=across,
            device_id_type=MESH,
        )

    def shift(i):
        return pltpu.make_async_remote_copy(
            src_ref=bc.at[i],
            dst_ref=bo.at[i],
            send_sem=z_send.at[i],
            recv_sem=z_recv.at[i],
            device_id=across,
            device_id_type=MESH,
        )

    def state(i):
        return pltpu.make_async_remote_copy(
            src_ref=pout.at[i],
            dst_ref=pin.at[i],
            send_sem=y_send.at[i],
            recv_sem=y_recv.at[i],
            device_id={"tm_0": jnp.minimum(y + 1, NYD - 1)},
            device_id_type=MESH,
        )

    def swapped_end(i):
        return pltpu.make_async_remote_copy(
            src_ref=p.at[HALF * (1 - core) + i],
            dst_ref=eo.at[i],
            send_sem=s_send.at[i],
            recv_sem=s_recv.at[i],
            device_id=beside,
            device_id_type=MESH,
        )

    begin(rims())
    lists.wait()

    def traffic(n):
        @pl.when(n == 0)
        def _():
            block_wait(0, 0)
            block_start(0, 1)

        @pl.when(n < LAST + 1)
        def _():
            block_wait(n + 1, 0)
            block_start(n + 1, 1)

        @pl.when(n == 1)
        def _():
            block_start(0, 2)

        @pl.when(n > 0)
        def _():
            block_start(n, 2)

        @pl.when(n < LAST)
        def _():
            block_start(n + 2, 0)

    def step(k, carry):
        def early_one():
            @pl.when(k > 0)
            def _():
                block_wait(2 * k, 1)

            traffic(2 * k)

            @pl.when(k == 0)
            def _():
                gp[...] = p[...]

        def early_two():
            @pl.when(k == 0)
            def _():
                block_wait(0, 1)
                block_wait(1, 1)

            @pl.when(k > 0)
            def _():
                block_wait(2 * k + 1, 1)

            traffic(2 * k + 1)

            for o in range(1, NZD):
                @pl.when(k == o)
                def _(o=o):
                    dealt(2, o).start()

            @pl.when(k == 5)
            def _():
                for o in range(1, NZD):
                    dealt(2, o).wait()
                factors(0).start()
                factors(1).start()

            @pl.when(k == 6)
            def _():
                factors(0).wait()
                factors(1).wait()
                factors_ready()
                scales().start()

            @pl.when(k == 7)
            def _():
                scales().wait()
                for i in range(HALF):
                    ay[i] = ac[i] * ao[i]

        def late_one():
            @pl.when(k == 0)
            def _():
                end(rims())

        two_sweeps(p, a, b, 0, True, early_one, late_one)
        two_sweeps(b, a, b, 1, False, early_two, lambda: None)
        block_wait(2 * k, 2)
        block_wait(2 * k + 1, 2)
        fix(k)
        return carry

    lax.fori_loop(0, INCREMENTS, step, 0)

    def returned(o):
        to = lax.rem(sz + o, NZD)
        return pltpu.make_async_remote_copy(
            src_ref=p.at[pl.ds(DEEP * to, DEEP)],
            dst_ref=back.at[:, own_rows, :],
            send_sem=o_send.at[o],
            recv_sem=o_recv.at[o],
            device_id={"sz": to},
            device_id_type=MESH,
        )

    for i in range(HALF):
        swapped_end(i).start()
    for i in range(HALF):
        swapped_end(i).wait()
        own = p[HALF * core + i]
        s0 = jnp.where(core == 0, own, eo[i]) - ga0[i]
        s1 = jnp.where(core == 0, eo[i], own) - ga1[i]
        b0[i] = s0
        bc[i] = a1[i] * s0 + s1
        shift(i).start()
    for o in range(1, NZD):
        returned(o).start()
    back[:, own_rows, :] = p[mine]

    def sent(slab, i, source):
        return pltpu.make_async_remote_copy(
            src_ref=(x0, x1)[slab].at[i],
            dst_ref=xback.at[i % DEEP, pl.ds(ROWS * quarter(source), ROWS), :],
            send_sem=x_send.at[slab, i],
            recv_sem=x_recv.at[source, i % DEEP],
            device_id={"tm_2": slab, "sz": 2 * core + i // DEEP},
            device_id_type=MESH,
        )

    def stays(slab, i):
        return jnp.logical_and(core == slab, sz == 2 * core + i // DEEP)

    for i in range(HALF):
        shift(i).wait()

        @pl.when(has_yl)
        def _(i=i):
            state(i).wait_recv()
            pout[i] = pin[i]

        before = pout[i]
        shift_0 = jnp.where(zh == 0, bc[i], bo[i])
        shift_1 = jnp.where(zh == 0, bo[i], bc[i])
        scale_0 = jnp.where(zh == 0, ac[i], ao[i])
        scale_1 = jnp.where(zh == 0, ao[i], ac[i])
        pout[i] = ay[i] * before + (scale_1 * shift_0 + shift_1)

        @pl.when(has_yr)
        def _(i=i):
            state(i).start()

        start = jnp.where(zh == 0, before, scale_0 * before + shift_0)
        x0[i] = start
        x1[i] = a0[i] * start + b0[i]
        for slab in range(2):
            @pl.when(jnp.logical_not(stays(slab, i)))
            def _(slab=slab, i=i):
                sent(slab, i, sz).start()

            @pl.when(stays(slab, i))
            def _(slab=slab, i=i):
                xback[i % DEEP, own_rows, :] = (x0, x1)[slab][i]

    for o in range(1, NZD):
        returned(o).wait()
    e_ref[0] = back[...]
    for slab in range(2):
        for i in range(HALF):
            @pl.when(jnp.logical_not(stays(slab, i)))
            def _(slab=slab, i=i):
                sent(slab, i, sz).wait_send()

    for t in range(NZD):
        @pl.when(jnp.logical_not(jnp.logical_and(core == sz // 2, sz == t)))
        def _(t=t):
            for i in range(DEEP):
                sent(0, i, t).wait_recv()

    for i in range(HALF):
        @pl.when(has_yr)
        def _(i=i):
            state(i).wait_send()

    x_ref[0] = xback[...]


def shards(g, c, f, d, ids, cnt, m):
    hbm = pl.BlockSpec(memory_space=pltpu.HBM)
    vm = pl.BlockSpec(memory_space=pltpu.VMEM)

    def f32(*shape):
        return pltpu.VMEM(shape, jnp.float32)

    field = f32(LAYERS, ROWS, NZ)
    brick = f32(DEEP, NY, NZ)
    part = f32(HALF, ROWS, NZ)
    xf = f32(2, 2, ROWS, NZ)
    zf = f32(2, 2, LAYERS, NZ)
    x1, z1 = f32(ROWS, NZ), f32(LAYERS, NZ)
    dma = pltpu.SemaphoreType.DMA
    out = jax.ShapeDtypeStruct(g.shape, jnp.float32)
    return pl.pallas_call(
        kernel,
        out_shape=(out, out),
        in_specs=[hbm] * 7,
        out_specs=(vm, vm),
        scratch_shapes=[field] * 9
        + [brick] * 2
        + [xf, xf, zf, zf, zf, zf, f32(2, 4, 8, NZ)]
        + [z1] * 6
        + [x1, x1, z1, z1] * 4
        + [
            f32(INCREMENTS, MAXT, TILE, TILE),
            pltpu.VMEM((INCREMENTS, MAXT), jnp.int32),
            pltpu.VMEM((1, INCREMENTS), jnp.int32),
            f32(INCREMENTS, NZD, PAIRS, TILE, 128),
            pltpu.VMEM((NZD, 2 * INCREMENTS, 128), jnp.int32),
            f32(128, 128),
        ]
        + [part] * 17
        + [
            pltpu.SMEM((NZD, 2 * INCREMENTS, 128), jnp.int32),
            dma((3, NZD)), dma((3, NZD)), dma((2, 3)), dma((2, 3)), dma((NZD,)), dma((NZD,)),
            dma((8, 2)), dma((8, 2)), dma((2, 4)), dma((2, 4)),
            dma((4, 2, 3)), dma((4, 2, 3)),
            dma((NZD,)), dma((NZD,)), dma((7,)),
            dma((2,)), dma((2,)), dma((HALF,)), dma((HALF,)), dma, dma, dma((HALF,)), dma((HALF,)),
            dma((HALF,)), dma((HALF,)), dma((2, HALF)), dma((NZD, DEEP)),
        ],
        compiler_params=pltpu.CompilerParams(
            collective_id=0, has_side_effects=True, vmem_limit_bytes=48 << 20
        ),
    )(g, c, f, d, ids, cnt.reshape(1, INCREMENTS), m)


def solution(mesh):
    split = Mesh(
        mesh.devices.reshape(8, 2, 2, NXD, NZD), ("tm_0", "tm_1", "tm_2", "sx", "sz")
    )
    return jax.shard_map(
        shards,
        mesh=split,
        in_specs=(
            P(TM, SPACE, None, None),
            P(SPACE, None, None),
            P(TM, SPACE, None, None),
            P(TM, SPACE, None, None),
            P(TM, SPACE),
            P(TM, SPACE),
            P(TM, SPACE, None, None),
        ),
        out_specs=(P(TM, SPACE, None, None), P(TM, SPACE, None, None)),
        check_vma=False,
    )
```

time: 229 us -> 196 us (0.86)
  Pallas kernels: 219 us -> 187 us
    pallas_call x1, Pallas kernels: 219 us -> 187 us  [shards(): pl.pallas_call(kernel, out_shape=(out, out), in_specs=[hbm] * 7, out_spec...]
    unnamed x15 -> x16, local copies, waits for them, and re-layouts: 8.76 us -> 8.68 us
where the time goes in v3:
time: 196 us
  Pallas kernels  187 us (95%)
  local copies, waits for them, and re-layouts  8.68 us (4%)
    pallas_call x1, Pallas kernels, shards(): pl.pallas_call(kernel, out_shape=(out, out), in_specs=[hbm] * 7, out_spec...  187 us
    unnamed x16, local copies, waits for them, and re-layouts  8.68 us

profile of v3, /device:TPU:121, one launch (start us, length us, event | category | flops | bytes accessed | tf_op | source)
XLA Modules:
  0.0 196.0 jit_solution(5920948992689232449)
XLA Ops:
  0.6 0.0 copy-start
  0.6 1.6 copy-done
  2.2 0.0 copy-start.1
  2.2 1.0 copy-done.1
  3.3 0.0 copy-start.2
  3.3 1.0 copy-done.2
  4.3 0.0 copy-start.3
  4.3 1.0 copy-done.3
  5.4 0.0 copy-start.4
  5.4 1.0 copy-done.4
  6.4 0.0 copy-start.5
  6.4 0.7 copy-done.5
  7.1 0.0 copy-start.6
  7.1 0.7 copy-done.6
  7.7 186.6 %shard_map.86 = (f32[1,4,128,256]{3,2,1,0:T(8,128)S(1)}, f32[1,4,128,256]{3,2,1,0:T(8,128)S(1)}) custom-call(f32[1,4,128,256]{3,2,1,0:T(8,128)S(1)} %copy-done.1, f32[4,128,256]{2,1,0:T(8,128)S(1)} %copy-done.2, f32[1,4,128,256]{3,2,1,0:T(8,128)S(1)} %copy-done.3, f32[1,4,128,256]{3,2,1,0:T(8,128)S(1)} %copy-done.4, s32[8,8]{1,0:T(8,128)S(1)} %copy-done.5, ...), custom_call_target="tpu_custom_call" | custom-call | tf_op jit(solution)/shard_map/pallas_call | solution.py:742
  194.4 0.8 copy.11
  195.2 0.8 copy.12
Async XLA Ops:
  0.6 1.6 copy-start
  2.2 1.0 copy-start.1
  3.3 1.0 copy-start.2
  4.3 1.0 copy-start.3
  5.4 1.0 copy-start.4
  6.4 0.7 copy-start.5
  7.1 0.7 copy-start.6
